TPU v7x, 32 devices: a whole 2x2x4 slice. The times are simulated.
32 devices in a mesh: pole: 2 (over x), wide: 8 (over z, y), narrow: 2 (over core).
Axes of the slice: x: 2, y: 2, z: 4, core: 2. Of those that a mesh axis runs over, the one named last changes fastest.
Arguments:
- h_panel: float32 [512, 2048], P(('pole', 'wide', 'narrow')), parts along dimension 0, may hold values from -0.3 to 0.3
- s_panel: float32 [512, 2048], P(('pole', 'wide', 'narrow')), parts along dimension 0, may hold values from -0.3 to 0.3
- col_index: int32 [512], P('pole'), parts along dimension 0, may hold values from 0 to 255, each once
- pattern: int32 [256], P(('pole', 'wide', 'narrow')), parts along dimension 0, may hold values 0 or 1
- dinv: float32 [512, 256], P('pole'), parts along dimension 0, may hold values from -4 to 4, as said below
- ainv_cc: float32 [4096, 8, 2, 128], P(('pole', 'wide'), None, 'narrow'), parts along dimension 0, may hold values from -1 to 1
Outputs:
- ainv_ck: float32 [4096, 256], P(('pole', 'wide'), 'narrow'), parts along dimension 0
- ainv_kk: float32 [512, 256], P(('pole', 'wide'), 'narrow'), parts along dimension 0
There are 2 independent parts, one for each index of `pole`. A program takes and returns all parts, laid end to end along the dimension named above; each array names one. Nothing has to cross between parts.
Inputs may be any that keep to these rules, and one draw needn't show every extreme that they name: `dinv`: diagonal entries between 0.25 and 4, off-diagonal entries at most 4 / sqrt(256) in magnitude.
All inputs are finite; a program needn't handle non-finite values. No bound on the sum of `pattern` on one device may be relied on, other than what follows from the above.
Results may differ from a plain program's by a relative error of at most 0.00011.
Values sent between devices are 32-bit elements; how exact they have to be, the bound alone decides.
No kernel may reach another device: no remote copies, remote signals or barrier semaphores. Data moves between devices by JAX's collectives and lax.ppermute only.
A program may use at most 64 MiB of HBM per device.

v0:
```python
import jax
import jax.numpy as jnp
from jax import lax
from jax.sharding import PartitionSpec as P

POLE_SHIFT = 0.5


def local(h_panel, s_panel, col_index, pattern, dinv, ainv_cc):
    panel_cols = h_panel - POLE_SHIFT * s_panel
    super_width = dinv.shape[0]
    received = lax.all_to_all(
        panel_cols, ("wide", "narrow"), split_axis=1, concat_axis=0, tiled=True
    )
    dinv_rows = jnp.take(dinv, col_index, axis=0)
    factor_panel = lax.dot_general(
        received,
        dinv_rows,
        (((0,), (0,)), ((), ())),
        precision=lax.Precision.HIGHEST,
        preferred_element_type=jnp.float32,
    )
    live_rows = (pattern > 0).astype(jnp.float32)
    factor_panel = (
        factor_panel.reshape(live_rows.shape[0], -1, super_width) * live_rows[:, None, None]
    ).reshape(factor_panel.shape)
    rows_here = ainv_cc.shape[0]
    inverse_flat = ainv_cc.reshape(rows_here, -1)
    partial_value = jnp.dot(
        inverse_flat,
        lax.all_gather(factor_panel, "wide", axis=0, tiled=True),
        precision=lax.Precision.HIGHEST,
        preferred_element_type=jnp.float32,
    )
    ainv_ck = -lax.psum_scatter(partial_value, "narrow", scatter_dimension=1, tiled=True)
    paired = lax.all_gather(factor_panel, "narrow", axis=0, tiled=True)
    corner_term = lax.dot_general(
        paired,
        ainv_ck,
        (((0,), (0,)), ((), ())),
        precision=lax.Precision.HIGHEST,
        preferred_element_type=jnp.float32,
    )
    summed = lax.psum_scatter(corner_term, "wide", scatter_dimension=0, tiled=True)
    half_width = ainv_ck.shape[1]
    rows_corner = summed.shape[0]
    corner = lax.dynamic_slice(
        dinv,
        (lax.axis_index("wide") * rows_corner, lax.axis_index("narrow") * half_width),
        (rows_corner, half_width),
    )
    return (ainv_ck, corner - summed)


def solution(mesh):
    placed = (
        P(("pole", "wide", "narrow"), None),
        P(("pole", "wide", "narrow"), None),
        P("pole"),
        P(("pole", "wide", "narrow")),
        P("pole", None),
        P(("pole", "wide"), None, "narrow", None),
    )
    return jax.shard_map(
        local,
        mesh=mesh,
        in_specs=placed,
        out_specs=(P(("pole", "wide"), "narrow"), P(("pole", "wide"), "narrow")),
        check_vma=False,
    )
```

profile of v0, /device:TPU:0, one launch (start us, length us, event | category | flops | bytes accessed | tf_op | source)
XLA Modules:
  0.0 148.3 jit_solution(7724145951328195672)
XLA Ops:
  7.2 0.0 copy-start
  7.2 1.7 %copy_bitcast_fusion = f32[16,16,128]{2,0,1:T(8,128)} fusion(f32[16,2048]{1,0:T(8,128)} %param.6, f32[16,2048]{1,0:T(8,128)} %param.7), kind=kLoop, calls=%fused_computation.7 | loop fusion | flops 65536 | bytes 393216 | tf_op jit(solution)/shard_map/all_to_all | solution.py:12
  8.9 0.0 copy-start.4
  8.9 7.5 %all-to-all-start = ((f32[16,16,128]{2,0,1:T(8,128)}), f32[16,16,128]{2,0,1:T(8,128)S(1)}, u32[]{:S(2)}, u32[]{:S(2)}) async-start(f32[16,16,128]{2,0,1:T(8,128)} %copy_bitcast_fusion), calls=%async_computation | async-start | bytes 262144 | tf_op jit(solution)/shard_map/all_to_all | solution.py:12
  16.4 0.0 copy-start.5
  16.4 0.0 all-gather.2.cloned.1.call-start
  16.5 0.0 copy-done.4
  16.5 0.6 copy-done.5
  17.1 0.0 copy-done
  17.1 0.0 copy-start.2
  17.1 1.0 gather_fusion
  18.1 6.2 %all-to-all-done = f32[16,16,128]{2,0,1:T(8,128)S(1)} async-done(((f32[16,16,128]{2,0,1:T(8,128)}), f32[16,16,128]{2,0,1:T(8,128)S(1)}, u32[]{:S(2)}, u32[]{:S(2)}) %all-to-all-start) | async-done | bytes 131104 | tf_op jit(solution)/shard_map/all_to_all | solution.py:12
  24.3 0.1 copy.16
  24.4 1.0 convolution_multiply_fusion
  25.4 0.0 all-gather.2.cloned.1.call-update
  25.5 0.0 reduce-scatter.3.cloned.1.call-start
  25.5 38.2 %all-gather.2.cloned.1.call-done = f32[1024,256]{1,0:T(8,128)} async-done(((f32[128,256]{1,0:T(8,128)}), f32[1024,256]{1,0:T(8,128)}) %all-gather.2.cloned.1.call-update) | async-done | bytes 1048592 | tf_op jit(solution)/shard_map/all_gather | solution.py:31
  63.7 0.0 copy-done.2
  63.7 3.8 %convolution_bitcast_fusion = f32[256,256]{0,1:T(8,128)} fusion(f32[1024,256]{1,0:T(8,128)} %all-gather.2.cloned.1.call-done, f32[32,8,8,128]{3,2,1,0:T(8,128)S(1)} %bitcast.28), kind=kOutput, calls=%fused_computation.1 | convolution fusion | flops 805306368 | bytes 2359296 | tf_op jit(solution)/shard_map/dot_general | solution.py:29
  67.5 0.0 copy-start.1
  67.5 0.0 reduce-scatter.3.cloned.1.call-update
  67.5 0.0 reduce-scatter.5.cloned.1.call-start
  67.5 0.8 copy-done.1
  68.4 2.0 %all_gather.7 = f32[256,256]{1,0:T(8,128)S(1)} all-gather(f32[128,256]{1,0:T(8,128)S(1)} %bitcast.27), channel_id=1, replica_groups=mesh['pole'=2,'wide'=8,'narrow'=2] {'narrow'}, dimensions={0}, use_global_device_ids=true | all-gather | bytes 393216 | tf_op jit(solution)/shard_map/all_gather | solution.py:36
  70.4 3.7 %reduce-scatter.3.cloned.1.call-done = f32[256,128]{0,1:T(8,128)} async-done(((f32[256,256]{0,1:T(8,128)}), f32[256,128]{0,1:T(8,128)}) %reduce-scatter.3.cloned.1.call-update) | async-done | bytes 131088 | tf_op jit(solution)/shard_map/reduce_scatter | solution.py:35
  74.1 2.2 %fusion.7 = f32[256,128]{1,0:T(8,128)} fusion(f32[256,256]{1,0:T(8,128)S(1)} %all_gather.7, f32[256,128]{0,1:T(8,128)} %reduce-scatter.3.cloned.1.call-done), kind=kOutput, calls=%fused_computation.17 | convolution fusion | flops 100696064 | bytes 524288 | tf_op jit(solution)/shard_map/dot_general | solution.py:37
  76.3 0.0 copy-start.3
  76.3 0.0 reduce-scatter.5.cloned.1.call-update
  76.3 0.9 copy-done.3
  77.2 0.8 copy.17
  77.9 62.5 %reduce-scatter.5.cloned.1.call-done = f32[32,128]{1,0:T(8,128)} async-done(((f32[256,128]{1,0:T(8,128)}), f32[32,128]{1,0:T(8,128)}) %reduce-scatter.5.cloned.1.call-update) | async-done | bytes 16400 | tf_op jit(solution)/shard_map/reduce_scatter | solution.py:44
  140.4 1.3 dynamic-slice_subtract_fusion
  (5 shorter events, 0.0 us)
Async XLA Ops:
  7.2 9.9 %copy-start = (f32[256,256]{1,0:T(8,128)S(1)}, f32[256,256]{1,0:T(8,128)}, u32[]{:S(2)}) copy-start(f32[256,256]{1,0:T(8,128)} %param.10) | copy-start | bytes 786436
  8.9 7.6 %copy-start.4 = (s32[256]{0:T(256)S(1)}, s32[256]{0:T(256)}, u32[]{:S(2)}) copy-start(s32[256]{0:T(256)} %param.8) | copy-start | bytes 3076
  8.9 15.5 %all-to-all-start = ((f32[16,16,128]{2,0,1:T(8,128)}), f32[16,16,128]{2,0,1:T(8,128)S(1)}, u32[]{:S(2)}, u32[]{:S(2)}) async-start(f32[16,16,128]{2,0,1:T(8,128)} %copy_bitcast_fusion), calls=%async_computation | async-start | bytes 262144 | tf_op jit(solution)/shard_map/all_to_all | solution.py:12
  16.4 0.7 copy-start.5
  16.4 47.2 %all-gather.2.cloned.1.call-start = ((), (), s32[]{:S(2)}) async-start(), calls=%async_computation.3 | async-start | bytes 1179648 | tf_op jit(solution)/shard_map/all_gather | solution.py:31
  17.1 46.6 %copy-start.2 = (f32[256,8,1,128]{3,2,1,0:T(1,128)S(1)}, f32[256,8,1,128]{3,2,1,0:T(1,128)}, u32[]{:S(2)}) copy-start(f32[256,8,1,128]{3,2,1,0:T(1,128)} %param.11) | copy-start | bytes 3145732
  25.5 48.6 %reduce-scatter.3.cloned.1.call-start = ((), (), s32[]{:S(2)}) async-start(), calls=%async_computation.4 | async-start | bytes 393216 | tf_op jit(solution)/shard_map/reduce_scatter | solution.py:35
  67.5 0.9 copy-start.1
  67.5 72.9 %reduce-scatter.5.cloned.1.call-start = ((), (), s32[]{:S(2)}) async-start(), calls=%async_computation.5 | async-start | bytes 147456 | tf_op jit(solution)/shard_map/reduce_scatter | solution.py:44
  76.3 0.9 copy-start.3
Sparse Core Ops, SparseCore 0:
  25.6 38.0 all-gather.1
  67.6 6.4 reduce-scatter.2
  77.4 62.9 reduce-scatter.4
where the time goes:
time: 149 us; the launch traced here: 148 us
  waiting for transfers between devices  111 us (74%)
  between operations  13.8 us (9%)
  starting transfers between devices  7.67 us (5%)
  matrix products  6.98 us (5%)
  local copies, waits for them, and re-layouts  4.11 us (3%)
  other arithmetic  3.04 us (2%)
  blocking collectives  1.98 us (1%)
    reduce_scatter x1, waiting for transfers between devices, local(): lax.psum_scatter(corner_term, 'wide', scatter_dimension=0, tiled=True)  62.5 us
    all_gather x1, waiting for transfers between devices, local(): lax.all_gather(factor_panel, 'wide', axis=0, tiled=True)  38.2 us
    all_to_all x1, starting transfers between devices, local(): lax.all_to_all(panel_cols, ('wide', 'narrow'), split_axis=1, concat_axis=...  7.55 us
    all_to_all x1, waiting for transfers between devices, local(): lax.all_to_all(panel_cols, ('wide', 'narrow'), split_axis=1, concat_axis=...  6.22 us
    dot_general x1, matrix products, local(): jnp.dot(inverse_flat, lax.all_gather(factor_panel, 'wide', axis=0, tiled=...  3.8 us
    reduce_scatter x1, waiting for transfers between devices, local(): lax.psum_scatter(partial_value, 'narrow', scatter_dimension=1, tiled=True)  3.75 us
    unnamed x13, local copies, waits for them, and re-layouts  3.05 us
  transfers between devices with their start and end apart: 4, of which 4 were waited for; matrix products, arithmetic and copies ran while one was open for 1% of the time, Pallas kernels for 0%

commit v1 on v0

v1 whole, which is shorter than its diff:
```python
import functools

import jax
import jax.numpy as jnp
from jax import lax
from jax.experimental import pallas as pl
from jax.experimental.pallas import tpu as pltpu
from jax.sharding import PartitionSpec as P

POLE_SHIFT = 0.5
LANES = 128
SUBLANES = 8
VMEM = pl.BlockSpec(memory_space=pltpu.VMEM)
SMEM = pl.BlockSpec(memory_space=pltpu.SMEM)


def split(x):
    high = x.astype(jnp.bfloat16)
    return high, (x - high.astype(jnp.float32)).astype(jnp.bfloat16)


def dot3(a, b, dims):
    one = functools.partial(
        lax.dot_general, dimension_numbers=(dims, ((), ())), preferred_element_type=jnp.float32
    )
    return one(a[0], b[0]) + (one(a[0], b[1]) + one(a[1], b[0]))


def call(kernel, outs, in_specs, args, flops, **more):
    shapes = [jax.ShapeDtypeStruct(*o) for o in outs]
    size = sum(x.size * x.dtype.itemsize for x in (*args, *shapes))
    return pl.pallas_call(
        kernel,
        out_shape=shapes,
        in_specs=in_specs,
        out_specs=[VMEM] * len(shapes),
        cost_estimate=pl.CostEstimate(flops=flops, bytes_accessed=size, transcendentals=0),
        **more,
    )(*args)


def prep_kernel(where, pattern, h, s, own, other, mask):
    core = where[1]
    columns = h.shape[0]
    bands = own.shape[0] // (h.shape[1] // (2 * LANES))
    blocks = own.shape[0] // bands
    for band in range(bands):
        low, high = band * SUBLANES, min(columns, (band + 1) * SUBLANES)
        for block in range(blocks):
            for out, half in ((own, core), (other, 1 - core)):
                at = pl.ds(pl.multiple_of((2 * block + half) * LANES, LANES), LANES)
                tile = h[low:high, at] - POLE_SHIFT * s[low:high, at]
                if high - low < SUBLANES:
                    tile = jnp.concatenate(
                        [tile, jnp.zeros((SUBLANES - high + low, LANES), jnp.float32)]
                    )
                out[band * blocks + block] = tile
    groups = pattern.shape[0]
    group = lax.broadcasted_iota(jnp.int32, (SUBLANES, LANES), 1) // (LANES // groups)
    live = jnp.zeros((SUBLANES, LANES), jnp.float32)
    for g in range(groups):
        live = jnp.where(group == g, (pattern[g] > 0).astype(jnp.float32), live)
    mask[0] = live


def ready_kernel(where, index, dinv, m, d_high, d_low, m_high, m_low):
    core = where[1]
    total, width = index.shape[0], dinv.shape[1]
    picked = (lax.broadcasted_iota(jnp.int32, (total, width), 1) == index[...]).astype(jnp.float32)
    half = width // 2
    for j, part in enumerate((core, 1 - core)):
        at = pl.ds(pl.multiple_of(part * half, LANES), half)
        rows = lax.dot_general(
            picked,
            dinv[:, at],
            (((1,), (0,)), ((), ())),
            precision=lax.Precision.HIGHEST,
            preferred_element_type=jnp.float32,
        )
        high, low = split(rows)
        d_high[:, j * half : (j + 1) * half] = high
        d_low[:, j * half : (j + 1) * half] = low
    for block in range(m.shape[1]):
        high, low = split(m[:, block, :])
        m_high[:, block * LANES : (block + 1) * LANES] = high
        m_low[:, block * LANES : (block + 1) * LANES] = low


def factor_kernel(count, where, d_high, d_low, *refs):
    parts, out = refs[:count], refs[count]
    chip, core = where[0], where[1]
    blocks = where.shape[0] - 2
    bands = (parts[0].shape[0] - 1) // blocks
    rows = jnp.concatenate([p[band * blocks + chip] for p in parts for band in range(bands)])
    rows = rows * parts[0][bands * blocks][:1, :]
    value = dot3((d_high[...], d_low[...]), split(rows), ((0,), (0,)))
    half = value.shape[0] // 2
    out[pl.ds(pl.multiple_of(core * half, SUBLANES), half), :] = value[:half]
    out[pl.ds(pl.multiple_of((1 - core) * half, SUBLANES), half), :] = value[half:]


def product_kernel(count, where, d_high, d_low, m_high, m_low, *refs):
    parts, (keep, send, live, p_high, p_low) = refs[:count], refs[count:]
    blocks = where.shape[0] - 2
    bands = (parts[0].shape[0] - 1) // blocks
    for k, part in enumerate(parts):
        live[pl.ds(where[2 + k], 1), :] = part[bands * blocks][:1, :]
    deep = bands * SUBLANES
    for block in range(blocks):
        row = live[block : block + 1, :]
        at = slice(block * LANES, (block + 1) * LANES)
        for k, part in enumerate(parts):
            rows = jnp.concatenate([part[band * blocks + block] for band in range(bands)]) * row
            high, low = split(rows)
            p_high[k * deep : (k + 1) * deep, at] = high
            p_low[k * deep : (k + 1) * deep, at] = low
    first = dot3((m_high[...], m_low[...]), (p_high[...], p_low[...]), ((1,), (1,)))
    both = dot3(split(first), (d_high[...], d_low[...]), ((1,), (0,)))
    half = both.shape[1] // 2
    keep[...] = both[:, :half]
    send[...] = both[:, half:]


def corner_kernel(where, keep, received, factor, factor_other, out, term):
    core = where[1]
    out[...] = -(keep[...] + received[...])
    half = out.shape[0] // 2
    for j, part in enumerate((core, 1 - core)):
        rows = out[pl.ds(pl.multiple_of(part * half, SUBLANES), half), :]
        value = dot3(split((factor, factor_other)[j][...]), split(rows), ((1,), (0,)))
        if j == 0:
            term[...] = value
        else:
            term[...] += value


def local(wides, h_panel, s_panel, col_index, pattern, dinv, ainv_cc):
    columns = h_panel.shape[0]
    rows_here, blocks, _, unit = ainv_cc.shape
    width = dinv.shape[0]
    deep = -(-columns // SUBLANES) * SUBLANES
    tiles = deep // SUBLANES * blocks
    wide, narrow = lax.axis_index("wide"), lax.axis_index("narrow")
    swap = [(0, 1), (1, 0)]

    ring = list(range(0, wides, 2)) + list(range(1, wides, 2))[::-1]
    place = [ring.index(i) for i in range(wides)]
    ahead = [(ring[i], ring[(i + 1) % wides]) for i in range(wides)]
    back = [(b, a) for a, b in ahead]
    offsets = [0]
    for step in range(1, (wides + 1) // 2):
        offsets += [-step, step]
    if wides % 2 == 0:
        offsets.append(-(wides // 2))
    table = jnp.array([[ring[(place[i] + o) % wides] for o in offsets] for i in range(wides)], jnp.int32)
    chips = lax.dynamic_index_in_dim(table, wide, 0, keepdims=False)
    where = jnp.concatenate([jnp.stack([wide, narrow]).astype(jnp.int32), chips])

    cuts = [(tiles, SUBLANES, LANES)] * 2 + [(1, SUBLANES, LANES)]
    own, other, mask = call(
        prep_kernel,
        [(c, jnp.float32) for c in cuts],
        [SMEM, SMEM, VMEM, VMEM],
        (where, pattern, h_panel, s_panel),
        2 * h_panel.size,
    )
    mine = jnp.concatenate([own, lax.ppermute(other, "narrow", swap), mask])

    parts = [mine]
    up = down = mine
    for step in range(1, (wides + 1) // 2):
        up = lax.ppermute(up, "wide", ahead)
        down = lax.ppermute(down, "wide", back)
        parts += [up, down]
    if wides % 2 == 0:
        parts.append(lax.ppermute(up, "wide", ahead))

    index = jnp.take(col_index.reshape(wides, 2, columns), chips, axis=0)
    index = jnp.where(narrow == 0, index, index[:, ::-1])
    index = jnp.pad(index, ((0, 0), (0, 0), (0, deep - columns))).reshape(-1, 1)
    total = index.shape[0]
    d_high, d_low, m_high, m_low = call(
        ready_kernel,
        [((total, width), jnp.bfloat16)] * 2 + [((rows_here, blocks * unit), jnp.bfloat16)] * 2,
        [SMEM, VMEM, VMEM, VMEM],
        (where, index, dinv, ainv_cc.reshape(rows_here, blocks, unit)),
        12 * total * width * width,
    )

    factor = call(
        functools.partial(factor_kernel, wides),
        [((width, unit), jnp.float32)],
        [SMEM] + [VMEM] * (2 + wides),
        (where, d_high, d_low, *parts),
        6 * total * width * unit,
    )[0]
    factor_other = lax.ppermute(factor, "narrow", swap)
    keep, send = call(
        functools.partial(product_kernel, wides),
        [((rows_here, width // 2), jnp.float32)] * 2,
        [SMEM] + [VMEM] * (4 + wides),
        (where, d_high, d_low, m_high, m_low, *parts),
        6 * total * rows_here * (blocks * unit + width),
        scratch_shapes=[pltpu.VMEM((blocks, unit), jnp.float32)]
        + [pltpu.VMEM((total, blocks * unit), jnp.bfloat16)] * 2,
    )
    received = lax.ppermute(send, "narrow", swap)
    ainv_ck, term = call(
        corner_kernel,
        [((rows_here, width // 2), jnp.float32), ((width, width // 2), jnp.float32)],
        [SMEM] + [VMEM] * 4,
        (where, keep, received, factor, factor_other),
        6 * width * width * rows_here,
    )
    share = width // wides
    shares = lax.all_to_all(term.reshape(wides, share, -1), "wide", 0, 0, tiled=True)
    corner = lax.dynamic_slice(dinv, (wide * share, narrow * (width // 2)), (share, width // 2))
    return ainv_ck, corner - jnp.sum(shares, axis=0)


def solution(mesh):
    placed = (
        P(("pole", "wide", "narrow"), None),
        P(("pole", "wide", "narrow"), None),
        P("pole"),
        P(("pole", "wide", "narrow")),
        P("pole", None),
        P(("pole", "wide"), None, "narrow", None),
    )
    return jax.shard_map(
        functools.partial(local, mesh.shape["wide"]),
        mesh=mesh,
        in_specs=placed,
        out_specs=(P(("pole", "wide"), "narrow"), P(("pole", "wide"), "narrow")),
        check_vma=False,
    )
```

time: 149 us -> 57.3 us (0.38)
  waiting for transfers between devices: 111 us -> 16 us
  Pallas kernels: 0 us -> 16.1 us
  between operations: 13.8 us -> 0.74 us
  matrix products: 6.98 us -> 0 us
  starting transfers between devices: 7.67 us -> 14.6 us
  blocking collectives: 1.98 us -> 0 us
  local copies, waits for them, and re-layouts: 4.11 us -> 5.74 us
    reduce_scatter x2 -> x0, waiting for transfers between devices: 66.2 us -> none  [the longest x1 62.5 us: local(): lax.psum_scatter(corner_term, 'wide', scatter_dimension=0, tiled=True)]
    all_gather x1 -> x0, waiting for transfers between devices: 38.2 us -> none  [local(): lax.all_gather(factor_panel, 'wide', axis=0, tiled=True)]
    pallas_call x0 -> x5, Pallas kernels: none -> 16.1 us  [call(): pl.pallas_call(kernel, out_shape=shapes, in_specs=in_specs, out_specs=[VM...]
    ppermute x0 -> x10, starting transfers between devices: none -> 10.1 us  [the longest x3 6.46 us: local(): up = lax.ppermute(up, 'wide', ahead)]
    ppermute x0 -> x10, waiting for transfers between devices: none -> 8.48 us  [the longest x3 5 us: local(): up = lax.ppermute(up, 'wide', ahead)]
    dot_general x3 -> x0, matrix products: 6.98 us -> none  [the longest x1 3.8 us: local(): jnp.dot(inverse_flat, lax.all_gather(factor_panel, 'wide', axis=0, tiled=...]
    all_to_all x1, starting transfers between devices: 7.55 us -> 4.54 us  [local(): lax.all_to_all(term.reshape(wides, share, -1), 'wide', 0, 0, tiled=True)]
    all_gather x1 -> x0, blocking collectives: 1.98 us -> none  [local(): paired = lax.all_gather(factor_panel, 'narrow', axis=0, tiled=True)]
  transfers between devices with their start and end apart: 4 -> 11, of which waited for: 4 -> 7; matrix products, arithmetic and copies ran while one was open for 1% -> 7% of each run, Pallas kernels for 0% -> 16%
where the time goes in v1:
time: 57.3 us; the launch traced here: 56.7 us
  Pallas kernels  16.1 us (28%)
  waiting for transfers between devices  16 us (28%)
  starting transfers between devices  14.6 us (25%)
  local copies, waits for them, and re-layouts  5.74 us (10%)
  other arithmetic  3.49 us (6%)
  between operations  0.74 us (1%)
    pallas_call x5, Pallas kernels, call(): pl.pallas_call(kernel, out_shape=shapes, in_specs=in_specs, out_specs=[VM...  16.1 us
    all_to_all x1, waiting for transfers between devices, local(): lax.all_to_all(term.reshape(wides, share, -1), 'wide', 0, 0, tiled=True)  7.51 us
    ppermute x3, starting transfers between devices, local(): up = lax.ppermute(up, 'wide', ahead)  6.46 us
    ppermute x3, waiting for transfers between devices, local(): up = lax.ppermute(up, 'wide', ahead)  5 us
    all_to_all x1, starting transfers between devices, local(): lax.all_to_all(term.reshape(wides, share, -1), 'wide', 0, 0, tiled=True)  4.54 us
    unnamed x26, local copies, waits for them, and re-layouts  3.57 us
    ppermute x1, starting transfers between devices, local(): parts.append(lax.ppermute(up, 'wide', ahead))  2.14 us
    ppermute x3, waiting for transfers between devices, local(): down = lax.ppermute(down, 'wide', back)  2.01 us
  transfers between devices with their start and end apart: 11, of which 7 were waited for; matrix products, arithmetic and copies ran while one was open for 7% of the time, Pallas kernels for 16%

profile of v1, /device:TPU:0, one launch (start us, length us, event | category | flops | bytes accessed | tf_op | source)
XLA Modules:
  0.0 56.7 jit_solution(12788861641553533724)
XLA Ops:
  0.6 0.7 %dynamic-slice_bitcast_fusion = s32[8]{0:T(128)S(1)} fusion(s32[8,8]{1,0:T(8,128)} %constant.39.clone, s32[]{:T(128)S(6)} %select_n.38), kind=kLoop, calls=%fused_computation.13 | loop fusion | bytes 68 | tf_op jit(solution)/shard_map/jit(dynamic_index_in_dim)/squeeze | solution.py:156
  1.3 0.6 %pad_add_fusion.where = s32[10]{0:T(128)} fusion(s32[8]{0:T(128)S(1)} %dynamic-slice_bitcast_fusion, s32[1]{0:T(128)} %bitcast.1, s32[1]{0:T(128)} %bitcast), kind=kLoop, calls=%fused_computation.12 | loop fusion | flops 20 | bytes 80 | tf_op jit(solution)/shard_map/concatenate | solution.py:157
  1.9 1.7 %shard_map.87 = (f32[16,8,128]{2,1,0:T(8,128)}, f32[16,8,128]{2,1,0:T(8,128)}, f32[1,8,128]{2,1,0:T(8,128)}) custom-call(s32[10]{0:T(128)} %pad_add_fusion.where, s32[8]{0:T(128)} %pattern.1, f32[16,2048]{1,0:T(8,128)} %h.1, f32[16,2048]{1,0:T(8,128)} %s.1), custom_call_target="tpu_custom_call" | custom-call | flops 65536 | bytes 397384 | tf_op jit(solution)/shard_map/pallas_call | solution.py:32
  3.6 0.5 collective-permute-start
  4.1 0.8 %constant_dynamic-update-slice_fusion.2 = f32[33,8,128]{2,1,0:T(8,128)S(1)} fusion(f32[16,8,128]{2,1,0:T(8,128)} %get-tuple-element.17), kind=kLoop, calls=%fused_computation.6 | loop fusion | bytes 131072
  4.9 0.3 collective-permute-done
  5.2 0.7 %copy-done.10 = f32[1,8,128]{2,1,0:T(8,128)S(1)} copy-done((f32[1,8,128]{2,1,0:T(8,128)S(1)}, f32[1,8,128]{2,1,0:T(8,128)}, u32[]{:S(2)}) %copy-start.10) | copy-done | bytes 4120
  5.9 2.9 %collective-permute-start.1 = (f32[33,8,128]{2,1,0:T(8,128)S(1)}, f32[33,8,128]{2,1,0:T(8,128)S(1)}, u32[]{:S(2)}, u32[]{:S(2)}) collective-permute-start(f32[33,8,128]{2,1,0:T(8,128)S(1)} %constant_dynamic-update-slice_fusion.refs_0_), channel_id=1, source_target_pairs={{0,4},{4,8},{8,12},{12,14},{14,10},{10,6},{6,2},{2,0},{1,5},{5,9},... | collective-permute-start | bytes 405512 | tf_op jit(solution)/shard_map/ppermute | solution.py:172
  8.8 0.7 %fusion = s32[8]{0:T(128)S(1)} fusion(s32[8,8]{1,0:T(8,128)} %constant.39.clone, s32[]{:T(128)S(6)} %select_n.38), kind=kLoop, calls=%fused_computation.11 | loop fusion | flops 24 | bytes 68 | tf_op jit(solution)/shard_map/jit(_take)/jit(_where)/select_n | solution.py:178
  9.5 3.2 %collective-permute-done.1.refs_1_ = f32[33,8,128]{2,1,0:T(8,128)S(1)} collective-permute-done((f32[33,8,128]{2,1,0:T(8,128)S(1)}, f32[33,8,128]{2,1,0:T(8,128)S(1)}, u32[]{:S(2)}, u32[]{:S(2)}) %collective-permute-start.1) | collective-permute-done | bytes 135200 | tf_op jit(solution)/shard_map/ppermute | solution.py:172
  12.7 1.8 %collective-permute-start.3 = (f32[33,8,128]{2,1,0:T(8,128)S(1)}, f32[33,8,128]{2,1,0:T(8,128)S(1)}, u32[]{:S(2)}, u32[]{:S(2)}) collective-permute-start(f32[33,8,128]{2,1,0:T(8,128)S(1)} %collective-permute-done.1.refs_1_), channel_id=1, source_target_pairs={{0,4},{4,8},{8,12},{12,14},{14,10},{10,6},{6,2},{2,0},{1,5},{5,9},... | collective-permute-start | bytes 405512 | tf_op jit(solution)/shard_map/ppermute | solution.py:172
  14.5 0.7 %copy-done.11 = s32[256]{0:T(256)S(1)} copy-done((s32[256]{0:T(256)S(1)}, s32[256]{0:T(256)}, u32[]{:S(2)}) %copy-start.11) | copy-done | bytes 1048
  15.2 0.6 %gather_fusion = s32[8,2,16]{2,1,0:T(2,128)S(1)} fusion(s32[8,2,16]{2,1,0:T(2,128)S(1)} %reshape.50, s32[1024]{0:T(1024)S(1)} %pad_clamp_fusion), kind=kCustom, calls=%fused_computation | custom fusion | bytes 2080 | tf_op jit(solution)/shard_map/jit(_take)/gather | solution.py:178
  15.8 0.7 %compare_and_fusion = pred[8]{0:T(512)(128)(4,1)S(1)} fusion(s32[8,8]{1,0:T(8,128)} %constant.39.clone, s32[]{:T(128)S(6)} %select_n.38), kind=kLoop, calls=%fused_computation.10 | loop fusion | flops 48 | bytes 44 | tf_op jit(solution)/shard_map/jit(_take)/and | solution.py:178
  16.5 0.3 collective-permute-start.4
  16.8 0.9 %collective-permute-done.3.refs_3_ = f32[33,8,128]{2,1,0:T(8,128)S(1)} collective-permute-done((f32[33,8,128]{2,1,0:T(8,128)S(1)}, f32[33,8,128]{2,1,0:T(8,128)S(1)}, u32[]{:S(2)}, u32[]{:S(2)}) %collective-permute-start.3) | collective-permute-done | bytes 135200 | tf_op jit(solution)/shard_map/ppermute | solution.py:172
  17.7 1.7 %collective-permute-start.5 = (f32[33,8,128]{2,1,0:T(8,128)S(1)}, f32[33,8,128]{2,1,0:T(8,128)S(1)}, u32[]{:S(2)}, u32[]{:S(2)}) collective-permute-start(f32[33,8,128]{2,1,0:T(8,128)S(1)} %collective-permute-done.3.refs_3_), channel_id=1, source_target_pairs={{0,4},{4,8},{8,12},{12,14},{14,10},{10,6},{6,2},{2,0},{1,5},{5,9},... | collective-permute-start | bytes 405512 | tf_op jit(solution)/shard_map/ppermute | solution.py:172
  19.6 2.0 %collective-permute-done.4.refs_4_ = f32[33,8,128]{2,1,0:T(8,128)S(1)} collective-permute-done((f32[33,8,128]{2,1,0:T(8,128)S(1)}, f32[33,8,128]{2,1,0:T(8,128)S(1)}, u32[]{:S(2)}, u32[]{:S(2)}) %collective-permute-start.4) | collective-permute-done | bytes 135200 | tf_op jit(solution)/shard_map/ppermute | solution.py:173
  21.8 0.9 %collective-permute-done.5.refs_5_ = f32[33,8,128]{2,1,0:T(8,128)S(1)} collective-permute-done((f32[33,8,128]{2,1,0:T(8,128)S(1)}, f32[33,8,128]{2,1,0:T(8,128)S(1)}, u32[]{:S(2)}, u32[]{:S(2)}) %collective-permute-start.5) | collective-permute-done | bytes 135200 | tf_op jit(solution)/shard_map/ppermute | solution.py:172
  22.7 2.1 %collective-permute-start.7 = (f32[33,8,128]{2,1,0:T(8,128)S(1)}, f32[33,8,128]{2,1,0:T(8,128)S(1)}, u32[]{:S(2)}, u32[]{:S(2)}) collective-permute-start(f32[33,8,128]{2,1,0:T(8,128)S(1)} %collective-permute-done.5.refs_5_), channel_id=1, source_target_pairs={{0,4},{4,8},{8,12},{12,14},{14,10},{10,6},{6,2},{2,0},{1,5},{5,9},... | collective-permute-start | bytes 405512 | tf_op jit(solution)/shard_map/ppermute | solution.py:176
  25.0 0.8 %reshape.62.index = s32[256,1]{1,0:T(8,128)} reshape(s32[8,2,16]{2,1,0:T(2,128)S(1)} %broadcast_select_fusion.1) | data formatting | bytes 2048 | tf_op jit(solution)/shard_map/reshape | solution.py:180
  25.7 6.7 %shard_map.86 = (bf16[256,256]{1,0:T(8,128)(2,1)}, bf16[256,256]{1,0:T(8,128)(2,1)}, bf16[256,1024]{1,0:T(8,128)(2,1)}, bf16[256,1024]{1,0:T(8,128)(2,1)}) custom-call(s32[10]{0:T(128)} %pad_add_fusion.where, s32[256,1]{1,0:T(8,128)} %reshape.62.index, f32[256,256]{1,0:T(8,128)} %dinv.1, f32[256,8,128]{2,1,0:T(8,128)} %bitcast.12), custom_call_target="tpu_custom_call" | custom-call | flops 201326592 | bytes 2622504 | tf_op jit(solution)/shard_map/pallas_call | solution.py:32
  32.5 0.6 %copy-done.6 = f32[33,8,128]{2,1,0:T(8,128)} copy-done((f32[33,8,128]{2,1,0:T(8,128)}, f32[33,8,128]{2,1,0:T(8,128)S(1)}, u32[]{:S(2)}) %copy-start.6) | copy-done | bytes 135192
  33.2 3.4 %shard_map.88 = (f32[256,128]{1,0:T(8,128)}, f32[256,128]{1,0:T(8,128)}) custom-call(s32[10]{0:T(128)} %pad_add_fusion.where, bf16[256,256]{1,0:T(8,128)(2,1)} %get-tuple-element.13.d_high, bf16[256,256]{1,0:T(8,128)(2,1)} %get-tuple-element.14.d_low, bf16[256,1024]{1,0:T(8,128)(2,1)} %get-tuple-element.15.m_high, ...), custom_call_target="tpu_custom_call" | custom-call | flops 503316480 | bytes 2654248 | tf_op jit(solution)/shard_map/pallas_call | solution.py:32
  36.6 2.3 %shard_map.89.factor = f32[256,128]{1,0:T(8,128)} custom-call(s32[10]{0:T(128)} %pad_add_fusion.where, bf16[256,256]{1,0:T(8,128)(2,1)} %get-tuple-element.13.d_high, bf16[256,256]{1,0:T(8,128)(2,1)} %get-tuple-element.14.d_low, f32[33,8,128]{2,1,0:T(8,128)} %copy-done, f32[33,8,128]{2,1,0:T(8,128)} %copy-done.1, f32[33,8,128]{2,1,0:T(8,128)} %copy-done.2, ...), custom_call_target="tpu_custom_call" | custom-call | flops 50331648 | bytes 1474600 | tf_op jit(solution)/shard_map/pallas_call | solution.py:32
  38.9 0.5 collective-permute-start.9
  39.5 1.2 %collective-permute-done.9.factor_other = f32[256,128]{1,0:T(8,128)S(1)} collective-permute-done((f32[256,128]{1,0:T(8,128)}, f32[256,128]{1,0:T(8,128)S(1)}, u32[]{:S(2)}, u32[]{:S(2)}) %collective-permute-start.9) | collective-permute-done | bytes 131104 | tf_op jit(solution)/shard_map/ppermute | solution.py:197
  40.7 0.6 %copy-done.9 = f32[256,128]{1,0:T(8,128)} copy-done((f32[256,128]{1,0:T(8,128)}, f32[256,128]{1,0:T(8,128)S(1)}, u32[]{:S(2)}) %copy-start.9) | copy-done | bytes 131096
  41.3 2.0 %shard_map.90 = (f32[256,128]{1,0:T(8,128)}, f32[256,128]{1,0:T(8,128)}) custom-call(s32[10]{0:T(128)} %pad_add_fusion.where, f32[256,128]{1,0:T(8,128)} %get-tuple-element.20.keep, f32[256,128]{1,0:T(8,128)} %copy-done.8, f32[256,128]{1,0:T(8,128)} %shard_map.89.factor, f32[256,128]{1,0:T(8,128)} %copy-done.9), custom_call_target="tpu_custom_call" | custom-call | flops 100663296 | bytes 786472 | tf_op jit(solution)/shard_map/pallas_call | solution.py:32
  43.3 4.5 %all-to-all-start = ((f32[8,32,128]{2,1,0:T(8,128)}), f32[8,32,128]{2,1,0:T(8,128)S(1)}, u32[]{:S(2)}, u32[]{:S(2)}) async-start(f32[8,32,128]{2,1,0:T(8,128)} %bitcast.13), calls=%async_computation | async-start | bytes 262144 | tf_op jit(solution)/shard_map/all_to_all | solution.py:216
  47.9 7.5 %all-to-all-done = f32[8,32,128]{2,1,0:T(8,128)S(1)} async-done(((f32[8,32,128]{2,1,0:T(8,128)}), f32[8,32,128]{2,1,0:T(8,128)S(1)}, u32[]{:S(2)}, u32[]{:S(2)}) %all-to-all-start) | async-done | bytes 131104 | tf_op jit(solution)/shard_map/all_to_all | solution.py:216
  55.4 1.3 %dynamic-slice_subtract_fusion = f32[32,128]{1,0:T(8,128)} fusion(f32[32,128]{1,0:T(8,128)S(1)} %reduce_sum.9, f32[256,256]{1,0:T(8,128)} %dinv.1, s32[]{:T(128)S(6)} %select_n.44, s32[]{:T(128)S(6)} %select_n.45), kind=kLoop, calls=%fused_computation.1 | loop fusion | flops 4096 | bytes 49160 | tf_op jit(solution)/shard_map/sub | solution.py:218
  (35 shorter events, 0.6 us)
Async XLA Ops:
  3.6 1.6 %collective-permute-start = (f32[16,8,128]{2,1,0:T(8,128)}, f32[16,8,128]{2,1,0:T(8,128)S(1)}, u32[]{:S(2)}, u32[]{:S(2)}) collective-permute-start(f32[16,8,128]{2,1,0:T(8,128)} %get-tuple-element.18), channel_id=1, source_target_pairs={{0,1},{1,0},{2,3},{3,2},{4,5},{5,4},{6,7},{7,6},{8,9},{9,8},{10,11... | collective-permute-start | bytes 196616 | tf_op jit(solution)/shard_map/ppermute | solution.py:167
  5.2 0.7 %copy-start.10 = (f32[1,8,128]{2,1,0:T(8,128)S(1)}, f32[1,8,128]{2,1,0:T(8,128)}, u32[]{:S(2)}) copy-start(f32[1,8,128]{2,1,0:T(8,128)} %get-tuple-element.19) | copy-start | bytes 12292
  5.9 26.6 %copy-start = (f32[33,8,128]{2,1,0:T(8,128)}, f32[33,8,128]{2,1,0:T(8,128)S(1)}, u32[]{:S(2)}) copy-start(f32[33,8,128]{2,1,0:T(8,128)S(1)} %constant_dynamic-update-slice_fusion.refs_0_) | copy-start | bytes 405508
  5.9 6.8 %collective-permute-start.1 = (f32[33,8,128]{2,1,0:T(8,128)S(1)}, f32[33,8,128]{2,1,0:T(8,128)S(1)}, u32[]{:S(2)}, u32[]{:S(2)}) collective-permute-start(f32[33,8,128]{2,1,0:T(8,128)S(1)} %constant_dynamic-update-slice_fusion.refs_0_), channel_id=1, source_target_pairs={{0,4},{4,8},{8,12},{12,14},{14,10},{10,6},{6,2},{2,0},{1,5},{5,9},... | collective-permute-start | bytes 405512 | tf_op jit(solution)/shard_map/ppermute | solution.py:172
  9.5 7.0 %collective-permute-start.2 = (f32[33,8,128]{2,1,0:T(8,128)S(1)}, f32[33,8,128]{2,1,0:T(8,128)S(1)}, u32[]{:S(2)}, u32[]{:S(2)}) collective-permute-start(f32[33,8,128]{2,1,0:T(8,128)S(1)} %constant_dynamic-update-slice_fusion.refs_0_), channel_id=1, source_target_pairs={{4,0},{8,4},{12,8},{14,12},{10,14},{6,10},{2,6},{0,2},{5,1},{9,5},... | collective-permute-start | bytes 405512 | tf_op jit(solution)/shard_map/ppermute | solution.py:173
  12.7 19.8 %copy-start.1 = (f32[33,8,128]{2,1,0:T(8,128)}, f32[33,8,128]{2,1,0:T(8,128)S(1)}, u32[]{:S(2)}) copy-start(f32[33,8,128]{2,1,0:T(8,128)S(1)} %collective-permute-done.1.refs_1_) | copy-start | bytes 405508
  12.7 5.1 %collective-permute-start.3 = (f32[33,8,128]{2,1,0:T(8,128)S(1)}, f32[33,8,128]{2,1,0:T(8,128)S(1)}, u32[]{:S(2)}, u32[]{:S(2)}) collective-permute-start(f32[33,8,128]{2,1,0:T(8,128)S(1)} %collective-permute-done.1.refs_1_), channel_id=1, source_target_pairs={{0,4},{4,8},{8,12},{12,14},{14,10},{10,6},{6,2},{2,0},{1,5},{5,9},... | collective-permute-start | bytes 405512 | tf_op jit(solution)/shard_map/ppermute | solution.py:172
  14.5 0.7 %copy-start.11 = (s32[256]{0:T(256)S(1)}, s32[256]{0:T(256)}, u32[]{:S(2)}) copy-start(s32[256]{0:T(256)} %param.9) | copy-start | bytes 3076
  16.5 16.0 %copy-start.2 = (f32[33,8,128]{2,1,0:T(8,128)}, f32[33,8,128]{2,1,0:T(8,128)S(1)}, u32[]{:S(2)}) copy-start(f32[33,8,128]{2,1,0:T(8,128)S(1)} %collective-permute-done.2.refs_2_) | copy-start | bytes 405508
  16.5 5.1 %collective-permute-start.4 = (f32[33,8,128]{2,1,0:T(8,128)S(1)}, f32[33,8,128]{2,1,0:T(8,128)S(1)}, u32[]{:S(2)}, u32[]{:S(2)}) collective-permute-start(f32[33,8,128]{2,1,0:T(8,128)S(1)} %collective-permute-done.2.refs_2_), channel_id=1, source_target_pairs={{4,0},{8,4},{12,8},{14,12},{10,14},{6,10},{2,6},{0,2},{5,1},{9,5},... | collective-permute-start | bytes 405512 | tf_op jit(solution)/shard_map/ppermute | solution.py:173
  17.7 14.7 %copy-start.3 = (f32[33,8,128]{2,1,0:T(8,128)}, f32[33,8,128]{2,1,0:T(8,128)S(1)}, u32[]{:S(2)}) copy-start(f32[33,8,128]{2,1,0:T(8,128)S(1)} %collective-permute-done.3.refs_3_) | copy-start | bytes 405508
  17.7 5.0 %collective-permute-start.5 = (f32[33,8,128]{2,1,0:T(8,128)S(1)}, f32[33,8,128]{2,1,0:T(8,128)S(1)}, u32[]{:S(2)}, u32[]{:S(2)}) collective-permute-start(f32[33,8,128]{2,1,0:T(8,128)S(1)} %collective-permute-done.3.refs_3_), channel_id=1, source_target_pairs={{0,4},{4,8},{8,12},{12,14},{14,10},{10,6},{6,2},{2,0},{1,5},{5,9},... | collective-permute-start | bytes 405512 | tf_op jit(solution)/shard_map/ppermute | solution.py:172
  21.6 10.9 %copy-start.4 = (f32[33,8,128]{2,1,0:T(8,128)}, f32[33,8,128]{2,1,0:T(8,128)S(1)}, u32[]{:S(2)}) copy-start(f32[33,8,128]{2,1,0:T(8,128)S(1)} %collective-permute-done.4.refs_4_) | copy-start | bytes 405508
  21.6 10.9 %collective-permute-start.6 = (f32[33,8,128]{2,1,0:T(8,128)S(1)}, f32[33,8,128]{2,1,0:T(8,128)S(1)}, u32[]{:S(2)}, u32[]{:S(2)}) collective-permute-start(f32[33,8,128]{2,1,0:T(8,128)S(1)} %collective-permute-done.4.refs_4_), channel_id=1, source_target_pairs={{4,0},{8,4},{12,8},{14,12},{10,14},{6,10},{2,6},{0,2},{5,1},{9,5},... | collective-permute-start | bytes 405512 | tf_op jit(solution)/shard_map/ppermute | solution.py:173
  22.7 9.7 %copy-start.5 = (f32[33,8,128]{2,1,0:T(8,128)}, f32[33,8,128]{2,1,0:T(8,128)S(1)}, u32[]{:S(2)}) copy-start(f32[33,8,128]{2,1,0:T(8,128)S(1)} %collective-permute-done.5.refs_5_) | copy-start | bytes 405508
  22.7 9.8 %collective-permute-start.7 = (f32[33,8,128]{2,1,0:T(8,128)S(1)}, f32[33,8,128]{2,1,0:T(8,128)S(1)}, u32[]{:S(2)}, u32[]{:S(2)}) collective-permute-start(f32[33,8,128]{2,1,0:T(8,128)S(1)} %collective-permute-done.5.refs_5_), channel_id=1, source_target_pairs={{0,4},{4,8},{8,12},{12,14},{14,10},{10,6},{6,2},{2,0},{1,5},{5,9},... | collective-permute-start | bytes 405512 | tf_op jit(solution)/shard_map/ppermute | solution.py:176
  32.5 0.7 %copy-start.6 = (f32[33,8,128]{2,1,0:T(8,128)}, f32[33,8,128]{2,1,0:T(8,128)S(1)}, u32[]{:S(2)}) copy-start(f32[33,8,128]{2,1,0:T(8,128)S(1)} %collective-permute-done.6.refs_6_) | copy-start | bytes 405508
  32.5 0.7 %copy-start.7 = (f32[33,8,128]{2,1,0:T(8,128)}, f32[33,8,128]{2,1,0:T(8,128)S(1)}, u32[]{:S(2)}) copy-start(f32[33,8,128]{2,1,0:T(8,128)S(1)} %collective-permute-done.7.refs_7_) | copy-start | bytes 405508
  36.6 2.8 %collective-permute-start.8 = (f32[256,128]{1,0:T(8,128)}, f32[256,128]{1,0:T(8,128)S(1)}, u32[]{:S(2)}, u32[]{:S(2)}) collective-permute-start(f32[256,128]{1,0:T(8,128)} %get-tuple-element.21), channel_id=1, source_target_pairs={{0,1},{1,0},{2,3},{3,2},{4,5},{5,4},{6,7},{7,6},{8,9},{9,8},{10,11... | collective-permute-start | bytes 393224 | tf_op jit(solution)/shard_map/ppermute | solution.py:207
  38.9 1.7 %collective-permute-start.9 = (f32[256,128]{1,0:T(8,128)}, f32[256,128]{1,0:T(8,128)S(1)}, u32[]{:S(2)}, u32[]{:S(2)}) collective-permute-start(f32[256,128]{1,0:T(8,128)} %shard_map.89.factor), channel_id=1, source_target_pairs={{0,1},{1,0},{2,3},{3,2},{4,5},{5,4},{6,7},{7,6},{8,9},{9,8},{10,11... | collective-permute-start | bytes 393224 | tf_op jit(solution)/shard_map/ppermute | solution.py:197
  39.5 1.2 %copy-start.8 = (f32[256,128]{1,0:T(8,128)}, f32[256,128]{1,0:T(8,128)S(1)}, u32[]{:S(2)}) copy-start(f32[256,128]{1,0:T(8,128)S(1)} %collective-permute-done.8.received) | copy-start | bytes 393220
  40.7 0.7 %copy-start.9 = (f32[256,128]{1,0:T(8,128)}, f32[256,128]{1,0:T(8,128)S(1)}, u32[]{:S(2)}) copy-start(f32[256,128]{1,0:T(8,128)S(1)} %collective-permute-done.9.factor_other) | copy-start | bytes 393220
  43.3 12.0 %all-to-all-start = ((f32[8,32,128]{2,1,0:T(8,128)}), f32[8,32,128]{2,1,0:T(8,128)S(1)}, u32[]{:S(2)}, u32[]{:S(2)}) async-start(f32[8,32,128]{2,1,0:T(8,128)} %bitcast.13), calls=%async_computation | async-start | bytes 262144 | tf_op jit(solution)/shard_map/all_to_all | solution.py:216

commit v2 on v1

v2 whole, which is shorter than its diff:
```python
import functools

import jax
import jax.numpy as jnp
from jax import lax
from jax.experimental import pallas as pl
from jax.experimental.pallas import tpu as pltpu
from jax.sharding import PartitionSpec as P

POLE_SHIFT = 0.5
LANES = 128
SUBLANES = 8
VMEM_LIMIT = 24 * 2**20
VMEM = pl.BlockSpec(memory_space=pltpu.VMEM)
HBM = pl.BlockSpec(memory_space=pltpu.HBM)


def split(x):
    high = x.astype(jnp.bfloat16)
    return high, (x - high.astype(jnp.float32)).astype(jnp.bfloat16)


def dot3(a, b, dims):
    one = functools.partial(
        lax.dot_general, dimension_numbers=(dims, ((), ())), preferred_element_type=jnp.float32
    )
    return one(a[0], b[0]) + (one(a[0], b[1]) + one(a[1], b[0]))


def call(kernel, outs, in_specs, args, flops, scratch=()):
    shapes = [jax.ShapeDtypeStruct(*o) for o in outs]
    size = sum(x.size * x.dtype.itemsize for x in (*args, *shapes))
    return pl.pallas_call(
        kernel,
        out_shape=shapes,
        in_specs=in_specs,
        out_specs=[VMEM] * len(shapes),
        scratch_shapes=scratch,
        cost_estimate=pl.CostEstimate(flops=flops, bytes_accessed=size, transcendentals=0),
        compiler_params=pltpu.CompilerParams(vmem_limit_bytes=VMEM_LIMIT),
    )(*args)


def in_hbm(x):
    return pltpu.with_memory_space_constraint(x, pltpu.HBM)


def chip_at(place, wides):
    return jnp.where(place < (wides + 1) // 2, 2 * place, 2 * (wides - 1 - place) + 1)


def place_of(chip, wides):
    return jnp.where(chip % 2 == 0, chip // 2, wides - 1 - chip // 2)


def offsets(wides):
    found = [0]
    for step in range(1, (wides + 1) // 2):
        found += [-step, step]
    if wides % 2 == 0:
        found.append(-(wides // 2))
    return found


def prep_kernel(pattern, h, s, own, other, flags, h_here, s_here, flag_sem, sems):
    core = lax.axis_index("narrow")
    columns = h.shape[0]
    tiles = other.shape[0]
    blocks = h.shape[1] // (2 * LANES)
    bands = tiles // blocks
    reads = []
    for band in range(bands):
        at = pl.ds(band * SUBLANES, min(columns - band * SUBLANES, SUBLANES))
        reads.append(
            [
                pltpu.make_async_copy(a.at[at], b.at[at], sems.at[i, band])
                for i, (a, b) in enumerate(((h, h_here), (s, s_here)))
            ]
        )
    live_read = pltpu.make_async_copy(pattern, flags, flag_sem)
    for pair in reads:
        for read in pair:
            read.start()
    live_read.start()
    for band in range(bands):
        for read in reads[band]:
            read.wait()
        low, high = band * SUBLANES, min(columns, (band + 1) * SUBLANES)
        for out, half in ((other, 1 - core), (own, core)):
            for block in range(blocks):
                at = pl.ds(pl.multiple_of((2 * block + half) * LANES, LANES), LANES)
                tile = h_here[low:high, at] - POLE_SHIFT * s_here[low:high, at]
                if high - low < SUBLANES:
                    rest = jnp.zeros((SUBLANES - high + low, LANES), jnp.float32)
                    tile = jnp.concatenate([tile, rest])
                out[band * blocks + block] = tile
    live_read.wait()
    groups = pattern.shape[0]
    group = lax.broadcasted_iota(jnp.int32, (SUBLANES, LANES), 1) // (LANES // groups)
    live = jnp.zeros((SUBLANES, LANES), jnp.float32)
    for g in range(groups):
        live = jnp.where(group == g, (flags[g] > 0).astype(jnp.float32), live)
    own[2 * tiles] = live


def inverse_kernel(m, high, low, here, sems):
    reads = [
        pltpu.make_async_copy(m.at[:, b, :], here.at[:, pl.ds(b * LANES, LANES)], sems.at[b])
        for b in range(m.shape[1])
    ]
    for read in reads:
        read.start()
    for b, read in enumerate(reads):
        read.wait()
        at = slice(b * LANES, (b + 1) * LANES)
        high[:, at], low[:, at] = split(here[:, at])


def pivot_kernel(wides, index, dinv, high, low, high_t, low_t, picked):
    core, place = lax.axis_index("narrow"), place_of(lax.axis_index("wide"), wides)
    total, width = picked.shape
    deep = total // (2 * wides)
    lane = lax.broadcasted_iota(jnp.int32, (deep, width), 1)
    for k, offset in enumerate(offsets(wides)):
        chip = chip_at((place + offset + wides) % wides, wides)
        for j, part in enumerate((core, 1 - core)):
            rows = index[pl.ds(pl.multiple_of((2 * chip + part) * deep, SUBLANES), deep), :]
            at = (2 * k + j) * deep
            picked[at : at + deep, :] = (lane == rows).astype(jnp.float32)
    half = width // 2
    chosen = picked[...].astype(jnp.bfloat16)
    for piece, out, out_t in zip(split(dinv[...]), (high, low), (high_t, low_t)):
        rows = jnp.dot(chosen, piece, preferred_element_type=jnp.float32)
        out_t[...] = rows.T.astype(jnp.bfloat16)
        rows = rows.astype(jnp.bfloat16)

        @pl.when(core == 0)
        def _():
            out[...] = rows

        @pl.when(core != 0)
        def _():
            out[:, :half] = rows[:, half:]
            out[:, half:] = rows[:, :half]


def factor_kernel(wides, high_t, low_t, *refs):
    parts, out = refs[:wides], refs[wides]
    chip = lax.axis_index("wide")
    bands = (parts[0].shape[0] - 1) // wides
    rows = jnp.concatenate([p[band * wides + chip] for p in parts for band in range(bands)])
    rows = rows * parts[0][bands * wides][:1, :]
    out[...] = dot3((high_t[...], low_t[...]), split(rows), ((1,), (0,)))


def product_kernel(wides, d_high, d_low, m_high, m_low, *refs):
    parts, (keep, send, live, p_high, p_low) = refs[:wides], refs[wides:]
    place = place_of(lax.axis_index("wide"), wides)
    bands = (parts[0].shape[0] - 1) // wides
    for part, offset in zip(parts, offsets(wides)):
        chip = chip_at((place + offset + wides) % wides, wides)
        live[pl.ds(chip, 1), :] = part[bands * wides][:1, :]
    deep = bands * SUBLANES
    for block in range(wides):
        row = live[block : block + 1, :]
        at = slice(block * LANES, (block + 1) * LANES)
        for k, part in enumerate(parts):
            rows = jnp.concatenate([part[band * wides + block] for band in range(bands)]) * row
            high, low = split(rows)
            p_high[k * deep : (k + 1) * deep, at] = high
            p_low[k * deep : (k + 1) * deep, at] = low
    first = dot3((m_high[...], m_low[...]), (p_high[...], p_low[...]), ((1,), (1,)))
    both = dot3(split(first), (d_high[...], d_low[...]), ((1,), (0,)))
    half = both.shape[1] // 2
    keep[...] = both[:, :half]
    send[...] = both[:, half:]


def corner_kernel(keep, received, factor, factor_other, term):
    core = lax.axis_index("narrow")
    half = keep.shape[0] // 2
    value = None
    for from_here, part in ((factor, core), (factor_other, 1 - core)):
        at = pl.ds(pl.multiple_of(part * half, SUBLANES), half)
        more = dot3(split(from_here[...]), split(keep[at, :] + received[at, :]), ((1,), (0,)))
        value = more if value is None else value + more
    term[...] = value


def local(wides, h_panel, s_panel, col_index, pattern, dinv, ainv_cc):
    columns, rows_all = h_panel.shape
    rows_here, blocks, _, unit = ainv_cc.shape
    width = dinv.shape[0]
    deep = -(-columns // SUBLANES) * SUBLANES
    tiles = deep // SUBLANES * blocks
    total = 2 * wides * deep
    wide, narrow = lax.axis_index("wide"), lax.axis_index("narrow")
    swap = [(0, 1), (1, 0)]
    f32, bf16 = jnp.float32, jnp.bfloat16
    ring = [*range(0, wides, 2), *range(1, wides, 2)[::-1]]
    ahead = [(ring[i], ring[(i + 1) % wides]) for i in range(wides)]
    back = [(b, a) for a, b in ahead]

    own, other = call(
        prep_kernel,
        [((2 * tiles + 1, SUBLANES, LANES), f32), ((tiles, SUBLANES, LANES), f32)],
        [HBM] * 3,
        tuple(in_hbm(x) for x in (pattern, h_panel, s_panel)),
        2 * h_panel.size,
        [
            pltpu.SMEM(pattern.shape, jnp.int32),
            pltpu.VMEM(h_panel.shape, f32),
            pltpu.VMEM(h_panel.shape, f32),
            pltpu.SemaphoreType.DMA(()),
            pltpu.SemaphoreType.DMA((2, deep // SUBLANES)),
        ],
    )
    mine = lax.dynamic_update_slice(own, lax.ppermute(other, "narrow", swap), (tiles, 0, 0))

    parts = [mine]
    up = down = mine
    for step in range(1, (wides + 1) // 2):
        up = lax.ppermute(up, "wide", ahead)
        down = lax.ppermute(down, "wide", back)
        parts += [up, down]
    if wides % 2 == 0:
        parts.append(lax.ppermute(up, "wide", ahead))

    m_high, m_low = call(
        inverse_kernel,
        [((rows_here, blocks * unit), bf16)] * 2,
        [HBM],
        (in_hbm(ainv_cc.reshape(rows_here, blocks, unit)),),
        4 * ainv_cc.size,
        [pltpu.VMEM((rows_here, blocks * unit), f32), pltpu.SemaphoreType.DMA((blocks,))],
    )
    index = jnp.pad(col_index.reshape(-1, columns), ((0, 0), (0, deep - columns))).reshape(-1, 1)
    d_high, d_low, d_high_t, d_low_t = call(
        functools.partial(pivot_kernel, wides),
        [((total, width), bf16)] * 2 + [((width, total), bf16)] * 2,
        [VMEM] * 2,
        (index, dinv),
        4 * total * width * width,
        [pltpu.VMEM((total, width), f32)],
    )
    factor = call(
        functools.partial(factor_kernel, wides),
        [((width, unit), f32)],
        [VMEM] * (2 + wides),
        (d_high_t, d_low_t, *parts),
        6 * total * width * unit,
    )[0]
    factor_other = lax.ppermute(factor, "narrow", swap)
    keep, send = call(
        functools.partial(product_kernel, wides),
        [((rows_here, width // 2), f32)] * 2,
        [VMEM] * (4 + wides),
        (d_high, d_low, m_high, m_low, *parts),
        6 * total * rows_here * (blocks * unit + width),
        [pltpu.VMEM((blocks, unit), f32)] + [pltpu.VMEM((total, blocks * unit), bf16)] * 2,
    )
    received = lax.ppermute(send, "narrow", swap)
    term = call(
        corner_kernel,
        [((width, width // 2), f32)],
        [VMEM] * 4,
        (keep, received, factor, factor_other),
        6 * width * width * rows_here,
    )[0]
    share = width // wides
    shares = lax.all_to_all(term.reshape(wides, share, -1), "wide", 0, 0, tiled=True)
    corner = lax.dynamic_slice(dinv, (wide * share, narrow * (width // 2)), (share, width // 2))
    return -(keep + received), corner + jnp.sum(shares, axis=0)


def solution(mesh):
    placed = (
        P(("pole", "wide", "narrow"), None),
        P(("pole", "wide", "narrow"), None),
        P("pole"),
        P(("pole", "wide", "narrow")),
        P("pole", None),
        P(("pole", "wide"), None, "narrow", None),
    )
    return jax.shard_map(
        functools.partial(local, mesh.shape["wide"]),
        mesh=mesh,
        in_specs=placed,
        out_specs=(P(("pole", "wide"), "narrow"), P(("pole", "wide"), "narrow")),
        check_vma=False,
    )
```

time: 57.3 us -> 43.8 us (0.76)
  Pallas kernels: 16.1 us -> 5.39 us
  local copies, waits for them, and re-layouts: 5.74 us -> 0.15 us
  waiting for transfers between devices: 16 us -> 19.2 us
  other arithmetic: 3.49 us -> 1.3 us
  starting transfers between devices: 14.6 us -> 16.7 us
    pallas_call x5 -> x6, Pallas kernels: 16.1 us -> 5.39 us  [call(): pl.pallas_call(kernel, out_shape=shapes, in_specs=in_specs, out_specs=[VM...]
    ppermute x3, waiting for transfers between devices: 5 us -> 9.85 us  [local(): up = lax.ppermute(up, 'wide', ahead)]
    unnamed x26 -> x4, local copies, waits for them, and re-layouts: 3.57 us -> 0.01 us
    ppermute x3, waiting for transfers between devices: 2.01 us -> 0.01 us  [local(): down = lax.ppermute(down, 'wide', back)]
    all_to_all x1, starting transfers between devices: 4.54 us -> 6.34 us  [local(): lax.all_to_all(term.reshape(wides, share, -1), 'wide', 0, 0, tiled=True)]
    sub x1 -> x0, other arithmetic: 1.34 us -> none  [local(): return (ainv_ck, corner - jnp.sum(shares, axis=0))]
    ppermute x1, waiting for transfers between devices: 1.19 us -> 0.01 us  [local(): factor_other = lax.ppermute(factor, 'narrow', swap)]
    ppermute x1, waiting for transfers between devices: 0.01 us -> 0.98 us  [local(): received = lax.ppermute(send, 'narrow', swap)]
  transfers between devices with their start and end apart: 11 -> 11, of which waited for: 7 -> 7; matrix products, arithmetic and copies ran while one was open for 7% -> 2% of each run, Pallas kernels for 16% -> 7%
where the time goes in v2:
time: 43.8 us; the launch traced here: 43.5 us
  waiting for transfers between devices  19.2 us (44%)
  starting transfers between devices  16.7 us (38%)
  Pallas kernels  5.39 us (12%)
  other arithmetic  1.3 us (3%)
  between operations  0.72 us (2%)
    ppermute x3, waiting for transfers between devices, local(): up = lax.ppermute(up, 'wide', ahead)  9.85 us
    all_to_all x1, waiting for transfers between devices, local(): lax.all_to_all(term.reshape(wides, share, -1), 'wide', 0, 0, tiled=True)  6.84 us
    ppermute x3, starting transfers between devices, local(): up = lax.ppermute(up, 'wide', ahead)  6.51 us
    all_to_all x1, starting transfers between devices, local(): lax.all_to_all(term.reshape(wides, share, -1), 'wide', 0, 0, tiled=True)  6.34 us
    pallas_call x6, Pallas kernels, call(): pl.pallas_call(kernel, out_shape=shapes, in_specs=in_specs, out_specs=[VM...  5.39 us
    ppermute x1, starting transfers between devices, local(): parts.append(lax.ppermute(up, 'wide', ahead))  2.16 us
    ppermute x1, waiting for transfers between devices, local(): received = lax.ppermute(send, 'narrow', swap)  0.98 us
    ppermute x1, waiting for transfers between devices, local(): lax.ppermute(other, 'narrow', swap)  0.9 us
  transfers between devices with their start and end apart: 11, of which 7 were waited for; matrix products, arithmetic and copies ran while one was open for 2% of the time, Pallas kernels for 7%

profile of v2, /device:TPU:0, one launch (start us, length us, event | category | flops | bytes accessed | tf_op | source)
XLA Modules:
  0.0 43.5 jit_solution(2344418819397184244)
XLA Ops:
  0.6 1.0 %shard_map.79 = (f32[33,8,128]{2,1,0:T(8,128)S(1)}, f32[16,8,128]{2,1,0:T(8,128)S(1)}) custom-call(s32[8]{0:T(128)} %pattern.1, f32[16,2048]{1,0:T(8,128)} %h.1, f32[16,2048]{1,0:T(8,128)} %s.1), custom_call_target="tpu_custom_call" | custom-call | flops 65536 | bytes 462880 | tf_op jit(solution)/shard_map/pallas_call | solution.py:33
  1.7 0.6 %collective-permute-start = (f32[16,8,128]{2,1,0:T(8,128)S(1)}, f32[16,8,128]{2,1,0:T(8,128)S(1)}, u32[]{:S(2)}, u32[]{:S(2)}) collective-permute-start(f32[16,8,128]{2,1,0:T(8,128)S(1)} %get-tuple-element.17), channel_id=1, source_target_pairs={{0,1},{1,0},{2,3},{3,2},{4,5},{5,4},{6,7},{7,6},{8,9},{9,8},{10,11... | collective-permute-start | bytes 196616 | tf_op jit(solution)/shard_map/ppermute | solution.py:218
  2.2 0.9 %collective-permute-done = f32[16,8,128]{2,1,0:T(8,128)S(1)} collective-permute-done((f32[16,8,128]{2,1,0:T(8,128)S(1)}, f32[16,8,128]{2,1,0:T(8,128)S(1)}, u32[]{:S(2)}, u32[]{:S(2)}) %collective-permute-start) | collective-permute-done | bytes 65568 | tf_op jit(solution)/shard_map/ppermute | solution.py:218
  3.1 3.0 %collective-permute-start.1 = (f32[33,8,128]{2,1,0:T(8,128)S(1)}, f32[33,8,128]{2,1,0:T(8,128)S(1)}, u32[]{:S(2)}, u32[]{:S(2)}) collective-permute-start(f32[33,8,128]{2,1,0:T(8,128)S(1)} %constant_dynamic-update-slice_fusion.refs_0_), channel_id=1, source_target_pairs={{0,4},{4,8},{8,12},{12,14},{14,10},{10,6},{6,2},{2,0},{1,5},{5,9},... | collective-permute-start | bytes 405512 | tf_op jit(solution)/shard_map/ppermute | solution.py:223
  6.1 0.0 collective-permute-start.2
  6.1 3.8 %collective-permute-done.1.refs_1_ = f32[33,8,128]{2,1,0:T(8,128)S(1)} collective-permute-done((f32[33,8,128]{2,1,0:T(8,128)S(1)}, f32[33,8,128]{2,1,0:T(8,128)S(1)}, u32[]{:S(2)}, u32[]{:S(2)}) %collective-permute-start.1) | collective-permute-done | bytes 135200 | tf_op jit(solution)/shard_map/ppermute | solution.py:223
  9.9 1.8 %collective-permute-start.3 = (f32[33,8,128]{2,1,0:T(8,128)S(1)}, f32[33,8,128]{2,1,0:T(8,128)S(1)}, u32[]{:S(2)}, u32[]{:S(2)}) collective-permute-start(f32[33,8,128]{2,1,0:T(8,128)S(1)} %collective-permute-done.1.refs_1_), channel_id=1, source_target_pairs={{0,4},{4,8},{8,12},{12,14},{14,10},{10,6},{6,2},{2,0},{1,5},{5,9},... | collective-permute-start | bytes 405512 | tf_op jit(solution)/shard_map/ppermute | solution.py:223
  11.7 0.0 collective-permute-done.2.refs_2_
  11.7 0.2 collective-permute-start.4
  12.0 3.0 %collective-permute-done.3.refs_3_ = f32[33,8,128]{2,1,0:T(8,128)S(1)} collective-permute-done((f32[33,8,128]{2,1,0:T(8,128)S(1)}, f32[33,8,128]{2,1,0:T(8,128)S(1)}, u32[]{:S(2)}, u32[]{:S(2)}) %collective-permute-start.3) | collective-permute-done | bytes 135200 | tf_op jit(solution)/shard_map/ppermute | solution.py:223
  15.0 1.7 %collective-permute-start.5 = (f32[33,8,128]{2,1,0:T(8,128)S(1)}, f32[33,8,128]{2,1,0:T(8,128)S(1)}, u32[]{:S(2)}, u32[]{:S(2)}) collective-permute-start(f32[33,8,128]{2,1,0:T(8,128)S(1)} %collective-permute-done.3.refs_3_), channel_id=1, source_target_pairs={{0,4},{4,8},{8,12},{12,14},{14,10},{10,6},{6,2},{2,0},{1,5},{5,9},... | collective-permute-start | bytes 405512 | tf_op jit(solution)/shard_map/ppermute | solution.py:223
  16.7 0.0 collective-permute-done.4.refs_4_
  16.8 0.3 collective-permute-start.6
  17.0 3.0 %collective-permute-done.5.refs_5_ = f32[33,8,128]{2,1,0:T(8,128)S(1)} collective-permute-done((f32[33,8,128]{2,1,0:T(8,128)S(1)}, f32[33,8,128]{2,1,0:T(8,128)S(1)}, u32[]{:S(2)}, u32[]{:S(2)}) %collective-permute-start.5) | collective-permute-done | bytes 135200 | tf_op jit(solution)/shard_map/ppermute | solution.py:223
  20.0 2.2 %collective-permute-start.7 = (f32[33,8,128]{2,1,0:T(8,128)S(1)}, f32[33,8,128]{2,1,0:T(8,128)S(1)}, u32[]{:S(2)}, u32[]{:S(2)}) collective-permute-start(f32[33,8,128]{2,1,0:T(8,128)S(1)} %collective-permute-done.5.refs_5_), channel_id=1, source_target_pairs={{0,4},{4,8},{8,12},{12,14},{14,10},{10,6},{6,2},{2,0},{1,5},{5,9},... | collective-permute-start | bytes 405512 | tf_op jit(solution)/shard_map/ppermute | solution.py:227
  22.2 0.1 copy.8.index
  22.3 0.0 copy-start
  22.3 1.4 %shard_map.78 = (bf16[256,1024]{1,0:T(8,128)(2,1)S(1)}, bf16[256,1024]{1,0:T(8,128)(2,1)S(1)}) custom-call(f32[256,8,128]{2,1,0:T(8,128)} %bitcast.3), custom_call_target="tpu_custom_call" | custom-call | flops 1048576 | bytes 2097152 | tf_op jit(solution)/shard_map/pallas_call | solution.py:33
  23.8 0.7 %shard_map.77 = (bf16[256,256]{1,0:T(8,128)(2,1)S(1)}, bf16[256,256]{1,0:T(8,128)(2,1)S(1)}, bf16[256,256]{1,0:T(8,128)(2,1)S(1)}, bf16[256,256]{1,0:T(8,128)(2,1)S(1)}) custom-call(s32[256,1]{1,0:T(8,128)S(1)} %copy.8.index, f32[256,256]{1,0:T(8,128)S(1)} %copy-done), custom_call_target="tpu_custom_call" | custom-call | flops 67108864 | bytes 787456 | tf_op jit(solution)/shard_map/pallas_call | solution.py:33
  24.4 0.0 collective-permute-done.6.refs_6_
  24.4 0.7 %collective-permute-done.7.refs_7_ = f32[33,8,128]{2,1,0:T(8,128)S(1)} collective-permute-done((f32[33,8,128]{2,1,0:T(8,128)S(1)}, f32[33,8,128]{2,1,0:T(8,128)S(1)}, u32[]{:S(2)}, u32[]{:S(2)}) %collective-permute-start.7) | collective-permute-done | bytes 135200 | tf_op jit(solution)/shard_map/ppermute | solution.py:227
  25.1 0.2 shard_map.81.factor
  25.4 0.1 collective-permute-start.9
  25.4 1.1 %shard_map.80 = (f32[256,128]{1,0:T(8,128)S(1)}, f32[256,128]{1,0:T(8,128)S(1)}) custom-call(bf16[256,256]{1,0:T(8,128)(2,1)S(1)} %get-tuple-element.12.d_high, bf16[256,256]{1,0:T(8,128)(2,1)S(1)} %get-tuple-element.13.d_low, bf16[256,1024]{1,0:T(8,128)(2,1)S(1)} %get-tuple-element.14.m_high, bf16[256,1024]{1,0:T(8,128)(2,1)S(1)} %get-tuple-element.15.m_low, ...), custom_call_target="tpu_custom_call" | custom-call | flops 503316480 | bytes 2654208 | tf_op jit(solution)/shard_map/pallas_call | solution.py:33
  26.6 0.6 %collective-permute-start.8 = (f32[256,128]{1,0:T(8,128)S(1)}, f32[256,128]{1,0:T(8,128)S(1)}, u32[]{:S(2)}, u32[]{:S(2)}) collective-permute-start(f32[256,128]{1,0:T(8,128)S(1)} %get-tuple-element.19), channel_id=1, source_target_pairs={{0,1},{1,0},{2,3},{3,2},{4,5},{5,4},{6,7},{7,6},{8,9},{9,8},{10,11... | collective-permute-start | bytes 393224 | tf_op jit(solution)/shard_map/ppermute | solution.py:262
  27.1 0.0 collective-permute-done.9.factor_other
  27.1 1.0 %collective-permute-done.8.received = f32[256,128]{1,0:T(8,128)S(1)} collective-permute-done((f32[256,128]{1,0:T(8,128)S(1)}, f32[256,128]{1,0:T(8,128)S(1)}, u32[]{:S(2)}, u32[]{:S(2)}) %collective-permute-start.8) | collective-permute-done | bytes 131104 | tf_op jit(solution)/shard_map/ppermute | solution.py:262
  28.1 0.9 %shard_map.82 = f32[256,128]{1,0:T(8,128)} custom-call(f32[256,128]{1,0:T(8,128)S(1)} %get-tuple-element.18.keep, f32[256,128]{1,0:T(8,128)S(1)} %collective-permute-done.8.received, f32[256,128]{1,0:T(8,128)S(1)} %shard_map.81.factor, f32[256,128]{1,0:T(8,128)S(1)} %collective-permute-done.9.factor_other), custom_call_target="tpu_custom_call" | custom-call | flops 100663296 | bytes 655360 | tf_op jit(solution)/shard_map/pallas_call | solution.py:33
  29.0 6.3 %all-to-all-start = ((f32[8,32,128]{2,1,0:T(8,128)}), f32[8,32,128]{2,1,0:T(8,128)S(1)}, u32[]{:S(2)}, u32[]{:S(2)}) async-start(f32[8,32,128]{2,1,0:T(8,128)} %bitcast.2), calls=%async_computation | async-start | bytes 262144 | tf_op jit(solution)/shard_map/all_to_all | solution.py:271
  35.4 0.7 %add_negate_fusion = f32[256,128]{1,0:T(8,128)} fusion(f32[256,128]{1,0:T(8,128)S(1)} %get-tuple-element.18.keep, f32[256,128]{1,0:T(8,128)S(1)} %collective-permute-done.8.received), kind=kLoop, calls=%fused_computation | loop fusion | flops 65536 | bytes 393216 | tf_op jit(solution)/shard_map/neg | solution.py:273
  36.0 6.8 %all-to-all-done = f32[8,32,128]{2,1,0:T(8,128)S(1)} async-done(((f32[8,32,128]{2,1,0:T(8,128)}), f32[8,32,128]{2,1,0:T(8,128)S(1)}, u32[]{:S(2)}, u32[]{:S(2)}) %all-to-all-start) | async-done | bytes 131104 | tf_op jit(solution)/shard_map/all_to_all | solution.py:271
  42.9 0.6 %dynamic-slice_add_fusion = f32[32,128]{1,0:T(8,128)} fusion(f32[32,128]{1,0:T(8,128)S(1)} %reduce_sum.9, f32[256,256]{1,0:T(8,128)S(1)} %copy-done, s32[]{:T(128)S(6)} %select_n.6, s32[]{:T(128)S(6)} %select_n.7), kind=kLoop, calls=%fused_computation.1 | loop fusion | flops 4096 | bytes 49160 | tf_op jit(solution)/shard_map/add | solution.py:273
  (5 shorter events, 0.0 us)
Async XLA Ops:
  1.7 1.5 %collective-permute-start = (f32[16,8,128]{2,1,0:T(8,128)S(1)}, f32[16,8,128]{2,1,0:T(8,128)S(1)}, u32[]{:S(2)}, u32[]{:S(2)}) collective-permute-start(f32[16,8,128]{2,1,0:T(8,128)S(1)} %get-tuple-element.17), channel_id=1, source_target_pairs={{0,1},{1,0},{2,3},{3,2},{4,5},{5,4},{6,7},{7,6},{8,9},{9,8},{10,11... | collective-permute-start | bytes 196616 | tf_op jit(solution)/shard_map/ppermute | solution.py:218
  3.1 19.0 %copy-start.1 = (s32[256]{0:T(256)S(1)}, s32[256]{0:T(256)}, u32[]{:S(2)}) copy-start(s32[256]{0:T(256)} %param.8) | copy-start | bytes 3076
  3.1 6.8 %collective-permute-start.1 = (f32[33,8,128]{2,1,0:T(8,128)S(1)}, f32[33,8,128]{2,1,0:T(8,128)S(1)}, u32[]{:S(2)}, u32[]{:S(2)}) collective-permute-start(f32[33,8,128]{2,1,0:T(8,128)S(1)} %constant_dynamic-update-slice_fusion.refs_0_), channel_id=1, source_target_pairs={{0,4},{4,8},{8,12},{12,14},{14,10},{10,6},{6,2},{2,0},{1,5},{5,9},... | collective-permute-start | bytes 405512 | tf_op jit(solution)/shard_map/ppermute | solution.py:223
  6.1 5.6 %collective-permute-start.2 = (f32[33,8,128]{2,1,0:T(8,128)S(1)}, f32[33,8,128]{2,1,0:T(8,128)S(1)}, u32[]{:S(2)}, u32[]{:S(2)}) collective-permute-start(f32[33,8,128]{2,1,0:T(8,128)S(1)} %constant_dynamic-update-slice_fusion.refs_0_), channel_id=1, source_target_pairs={{4,0},{8,4},{12,8},{14,12},{10,14},{6,10},{2,6},{0,2},{5,1},{9,5},... | collective-permute-start | bytes 405512 | tf_op jit(solution)/shard_map/ppermute | solution.py:224
  9.9 5.1 %collective-permute-start.3 = (f32[33,8,128]{2,1,0:T(8,128)S(1)}, f32[33,8,128]{2,1,0:T(8,128)S(1)}, u32[]{:S(2)}, u32[]{:S(2)}) collective-permute-start(f32[33,8,128]{2,1,0:T(8,128)S(1)} %collective-permute-done.1.refs_1_), channel_id=1, source_target_pairs={{0,4},{4,8},{8,12},{12,14},{14,10},{10,6},{6,2},{2,0},{1,5},{5,9},... | collective-permute-start | bytes 405512 | tf_op jit(solution)/shard_map/ppermute | solution.py:223
  11.7 5.0 %collective-permute-start.4 = (f32[33,8,128]{2,1,0:T(8,128)S(1)}, f32[33,8,128]{2,1,0:T(8,128)S(1)}, u32[]{:S(2)}, u32[]{:S(2)}) collective-permute-start(f32[33,8,128]{2,1,0:T(8,128)S(1)} %collective-permute-done.2.refs_2_), channel_id=1, source_target_pairs={{4,0},{8,4},{12,8},{14,12},{10,14},{6,10},{2,6},{0,2},{5,1},{9,5},... | collective-permute-start | bytes 405512 | tf_op jit(solution)/shard_map/ppermute | solution.py:224
  15.0 5.0 %collective-permute-start.5 = (f32[33,8,128]{2,1,0:T(8,128)S(1)}, f32[33,8,128]{2,1,0:T(8,128)S(1)}, u32[]{:S(2)}, u32[]{:S(2)}) collective-permute-start(f32[33,8,128]{2,1,0:T(8,128)S(1)} %collective-permute-done.3.refs_3_), channel_id=1, source_target_pairs={{0,4},{4,8},{8,12},{12,14},{14,10},{10,6},{6,2},{2,0},{1,5},{5,9},... | collective-permute-start | bytes 405512 | tf_op jit(solution)/shard_map/ppermute | solution.py:223
  16.8 7.7 %collective-permute-start.6 = (f32[33,8,128]{2,1,0:T(8,128)S(1)}, f32[33,8,128]{2,1,0:T(8,128)S(1)}, u32[]{:S(2)}, u32[]{:S(2)}) collective-permute-start(f32[33,8,128]{2,1,0:T(8,128)S(1)} %collective-permute-done.4.refs_4_), channel_id=1, source_target_pairs={{4,0},{8,4},{12,8},{14,12},{10,14},{6,10},{2,6},{0,2},{5,1},{9,5},... | collective-permute-start | bytes 405512 | tf_op jit(solution)/shard_map/ppermute | solution.py:224
  20.0 5.1 %collective-permute-start.7 = (f32[33,8,128]{2,1,0:T(8,128)S(1)}, f32[33,8,128]{2,1,0:T(8,128)S(1)}, u32[]{:S(2)}, u32[]{:S(2)}) collective-permute-start(f32[33,8,128]{2,1,0:T(8,128)S(1)} %collective-permute-done.5.refs_5_), channel_id=1, source_target_pairs={{0,4},{4,8},{8,12},{12,14},{14,10},{10,6},{6,2},{2,0},{1,5},{5,9},... | collective-permute-start | bytes 405512 | tf_op jit(solution)/shard_map/ppermute | solution.py:227
  22.3 1.5 %copy-start = (f32[256,256]{1,0:T(8,128)S(1)}, f32[256,256]{1,0:T(8,128)}, u32[]{:S(2)}) copy-start(f32[256,256]{1,0:T(8,128)} %dinv.1) | copy-start | bytes 786436
  25.4 1.8 %collective-permute-start.9 = (f32[256,128]{1,0:T(8,128)S(1)}, f32[256,128]{1,0:T(8,128)S(1)}, u32[]{:S(2)}, u32[]{:S(2)}) collective-permute-start(f32[256,128]{1,0:T(8,128)S(1)} %shard_map.81.factor), channel_id=1, source_target_pairs={{0,1},{1,0},{2,3},{3,2},{4,5},{5,4},{6,7},{7,6},{8,9},{9,8},{10,11... | collective-permute-start | bytes 393224 | tf_op jit(solution)/shard_map/ppermute | solution.py:253
  26.6 1.5 %collective-permute-start.8 = (f32[256,128]{1,0:T(8,128)S(1)}, f32[256,128]{1,0:T(8,128)S(1)}, u32[]{:S(2)}, u32[]{:S(2)}) collective-permute-start(f32[256,128]{1,0:T(8,128)S(1)} %get-tuple-element.19), channel_id=1, source_target_pairs={{0,1},{1,0},{2,3},{3,2},{4,5},{5,4},{6,7},{7,6},{8,9},{9,8},{10,11... | collective-permute-start | bytes 393224 | tf_op jit(solution)/shard_map/ppermute | solution.py:262
  29.0 13.9 %all-to-all-start = ((f32[8,32,128]{2,1,0:T(8,128)}), f32[8,32,128]{2,1,0:T(8,128)S(1)}, u32[]{:S(2)}, u32[]{:S(2)}) async-start(f32[8,32,128]{2,1,0:T(8,128)} %bitcast.2), calls=%async_computation | async-start | bytes 262144 | tf_op jit(solution)/shard_map/all_to_all | solution.py:271

commit v3 on v2

--- a/solution.py
+++ b/solution.py
@@ -200,6 +200,7 @@
     ring = [*range(0, wides, 2), *range(1, wides, 2)[::-1]]
     ahead = [(ring[i], ring[(i + 1) % wides]) for i in range(wides)]
     back = [(b, a) for a, b in ahead]
+    leap = [(2 * ring[i] + core, 2 * ring[(i + step) % wides] + core) for i in range(wides) for core, step in ((0, 2), (1, -2))]
 
     own, other = call(
         prep_kernel,
@@ -220,11 +221,13 @@
     parts = [mine]
     up = down = mine
     for step in range(1, (wides + 1) // 2):
+        if wides % 2 == 0 and step == wides // 2 - 1:
+            far = lax.ppermute(jnp.where(narrow == 0, up, down), ("wide", "narrow"), leap)
         up = lax.ppermute(up, "wide", ahead)
         down = lax.ppermute(down, "wide", back)
         parts += [up, down]
     if wides % 2 == 0:
-        parts.append(lax.ppermute(up, "wide", ahead))
+        parts.append(far)
 
     m_high, m_low = call(
         inverse_kernel,
@@ -268,9 +271,16 @@
         6 * width * width * rows_here,
     )[0]
     share = width // wides
-    shares = lax.all_to_all(term.reshape(wides, share, -1), "wide", 0, 0, tiled=True)
+    rest, near = term, 1
+    while near < wides:
+        mate = [(i, i ^ near) for i in range(wides)]
+        pieces = rest.reshape(-1, 2, share, rest.shape[-1])
+        side = (wide // near) % 2
+        sent = lax.ppermute(lax.dynamic_index_in_dim(pieces, 1 - side, 1, False), "wide", mate)
+        rest = (lax.dynamic_index_in_dim(pieces, side, 1, False) + sent).reshape(-1, rest.shape[-1])
+        near *= 2
     corner = lax.dynamic_slice(dinv, (wide * share, narrow * (width // 2)), (share, width // 2))
-    return -(keep + received), corner + jnp.sum(shares, axis=0)
+    return -(keep + received), corner + rest
 
 
 def solution(mesh):

time: 43.8 us -> 41.7 us (0.952)
  waiting for transfers between devices: 19.2 us -> 18 us
  Pallas kernels: 5.39 us -> 4.72 us
    ppermute x1 -> x4, waiting for transfers between devices: 0.66 us -> 8.1 us  [the longest x3 7.3 us: local(): lax.ppermute(lax.dynamic_index_in_dim(pieces, 1 - side, 1, False), 'wide'...]
    all_to_all x1 -> x0, waiting for transfers between devices: 6.84 us -> none  [local(): lax.all_to_all(term.reshape(wides, share, -1), 'wide', 0, 0, tiled=True)]
    all_to_all x1 -> x0, starting transfers between devices: 6.34 us -> none  [local(): lax.all_to_all(term.reshape(wides, share, -1), 'wide', 0, 0, tiled=True)]
    ppermute x1 -> x4, starting transfers between devices: 2.16 us -> 8.32 us  [the longest x3 5.51 us: local(): lax.ppermute(lax.dynamic_index_in_dim(pieces, 1 - side, 1, False), 'wide'...]
    ppermute x3, waiting for transfers between devices: 9.85 us -> 6.88 us  [local(): up = lax.ppermute(up, 'wide', ahead)]
    ppermute x3, waiting for transfers between devices: 0.01 us -> 1.16 us  [local(): down = lax.ppermute(down, 'wide', back)]
    pallas_call x6, Pallas kernels: 5.39 us -> 4.72 us  [call(): pl.pallas_call(kernel, out_shape=shapes, in_specs=in_specs, out_specs=[VM...]
    ppermute x1, starting transfers between devices: 0.55 us -> 0.07 us  [local(): received = lax.ppermute(send, 'narrow', swap)]
  transfers between devices with their start and end apart: 11 -> 13, of which waited for: 7 -> 10; matrix products, arithmetic and copies ran while one was open for 2% -> 2% of each run, Pallas kernels for 7% -> 6%
where the time goes in v3:
time: 41.7 us; the launch traced here: 41.5 us
  waiting for transfers between devices  18 us (43%)
  starting transfers between devices  16.5 us (40%)
  Pallas kernels  4.72 us (11%)
  other arithmetic  1.32 us (3%)
  between operations  0.76 us (2%)
    ppermute x3, waiting for transfers between devices, local(): lax.ppermute(lax.dynamic_index_in_dim(pieces, 1 - side, 1, False), 'wide'...  7.3 us
    ppermute x3, waiting for transfers between devices, local(): up = lax.ppermute(up, 'wide', ahead)  6.88 us
    ppermute x3, starting transfers between devices, local(): up = lax.ppermute(up, 'wide', ahead)  6.46 us
    ppermute x3, starting transfers between devices, local(): lax.ppermute(lax.dynamic_index_in_dim(pieces, 1 - side, 1, False), 'wide'...  5.51 us
    pallas_call x6, Pallas kernels, call(): pl.pallas_call(kernel, out_shape=shapes, in_specs=in_specs, out_specs=[VM...  4.72 us
    ppermute x1, starting transfers between devices, local(): lax.ppermute(jnp.where(narrow == 0, up, down), ('wide', 'narrow'), leap)  2.81 us
    ppermute x3, waiting for transfers between devices, local(): down = lax.ppermute(down, 'wide', back)  1.16 us
    ppermute x1, waiting for transfers between devices, local(): lax.ppermute(other, 'narrow', swap)  0.9 us
  transfers between devices with their start and end apart: 13, of which 10 were waited for; matrix products, arithmetic and copies ran while one was open for 2% of the time, Pallas kernels for 6%

profile of v3, /device:TPU:0, one launch (start us, length us, event | category | flops | bytes accessed | tf_op | source)
XLA Modules:
  0.0 41.5 jit_solution(12419701007756899751)
XLA Ops:
  0.6 1.0 %shard_map.79 = (f32[33,8,128]{2,1,0:T(8,128)S(1)}, f32[16,8,128]{2,1,0:T(8,128)S(1)}) custom-call(s32[8]{0:T(128)} %pattern.1, f32[16,2048]{1,0:T(8,128)} %h.1, f32[16,2048]{1,0:T(8,128)} %s.1), custom_call_target="tpu_custom_call" | custom-call | flops 65536 | bytes 462880 | tf_op jit(solution)/shard_map/pallas_call | solution.py:33
  1.7 0.6 %collective-permute-start = (f32[16,8,128]{2,1,0:T(8,128)S(1)}, f32[16,8,128]{2,1,0:T(8,128)S(1)}, u32[]{:S(2)}, u32[]{:S(2)}) collective-permute-start(f32[16,8,128]{2,1,0:T(8,128)S(1)} %get-tuple-element.17), channel_id=1, source_target_pairs={{0,1},{1,0},{2,3},{3,2},{4,5},{5,4},{6,7},{7,6},{8,9},{9,8},{10,11... | collective-permute-start | bytes 196616 | tf_op jit(solution)/shard_map/ppermute | solution.py:219
  2.2 0.9 %collective-permute-done = f32[16,8,128]{2,1,0:T(8,128)S(1)} collective-permute-done((f32[16,8,128]{2,1,0:T(8,128)S(1)}, f32[16,8,128]{2,1,0:T(8,128)S(1)}, u32[]{:S(2)}, u32[]{:S(2)}) %collective-permute-start) | collective-permute-done | bytes 65568 | tf_op jit(solution)/shard_map/ppermute | solution.py:219
  3.1 2.9 %collective-permute-start.1 = (f32[33,8,128]{2,1,0:T(8,128)S(1)}, f32[33,8,128]{2,1,0:T(8,128)S(1)}, u32[]{:S(2)}, u32[]{:S(2)}) collective-permute-start(f32[33,8,128]{2,1,0:T(8,128)S(1)} %constant_dynamic-update-slice_fusion.refs_0_), channel_id=1, source_target_pairs={{0,4},{4,8},{8,12},{12,14},{14,10},{10,6},{6,2},{2,0},{1,5},{5,9},... | collective-permute-start | bytes 405512 | tf_op jit(solution)/shard_map/ppermute | solution.py:226
  6.0 0.0 collective-permute-start.2
  6.0 3.8 %collective-permute-done.1.refs_1_ = f32[33,8,128]{2,1,0:T(8,128)S(1)} collective-permute-done((f32[33,8,128]{2,1,0:T(8,128)S(1)}, f32[33,8,128]{2,1,0:T(8,128)S(1)}, u32[]{:S(2)}, u32[]{:S(2)}) %collective-permute-start.1) | collective-permute-done | bytes 135200 | tf_op jit(solution)/shard_map/ppermute | solution.py:226
  9.9 1.8 %collective-permute-start.3 = (f32[33,8,128]{2,1,0:T(8,128)S(1)}, f32[33,8,128]{2,1,0:T(8,128)S(1)}, u32[]{:S(2)}, u32[]{:S(2)}) collective-permute-start(f32[33,8,128]{2,1,0:T(8,128)S(1)} %collective-permute-done.1.refs_1_), channel_id=1, source_target_pairs={{0,4},{4,8},{8,12},{12,14},{14,10},{10,6},{6,2},{2,0},{1,5},{5,9},... | collective-permute-start | bytes 405512 | tf_op jit(solution)/shard_map/ppermute | solution.py:226
  11.7 0.2 collective-permute-start.4
  11.9 3.0 %collective-permute-done.3.refs_3_ = f32[33,8,128]{2,1,0:T(8,128)S(1)} collective-permute-done((f32[33,8,128]{2,1,0:T(8,128)S(1)}, f32[33,8,128]{2,1,0:T(8,128)S(1)}, u32[]{:S(2)}, u32[]{:S(2)}) %collective-permute-start.3) | collective-permute-done | bytes 135200 | tf_op jit(solution)/shard_map/ppermute | solution.py:226
  15.0 1.7 %collective-permute-start.5 = (f32[33,8,128]{2,1,0:T(8,128)S(1)}, f32[33,8,128]{2,1,0:T(8,128)S(1)}, u32[]{:S(2)}, u32[]{:S(2)}) collective-permute-start(f32[33,8,128]{2,1,0:T(8,128)S(1)} %collective-permute-done.3.refs_3_), channel_id=1, source_target_pairs={{0,4},{4,8},{8,12},{12,14},{14,10},{10,6},{6,2},{2,0},{1,5},{5,9},... | collective-permute-start | bytes 405512 | tf_op jit(solution)/shard_map/ppermute | solution.py:226
  16.7 0.3 collective-permute-start.6
  17.0 2.8 %collective-permute-start.7 = (f32[33,8,128]{2,1,0:T(8,128)S(1)}, f32[33,8,128]{2,1,0:T(8,128)S(1)}, u32[]{:S(2)}, u32[]{:S(2)}) collective-permute-start(f32[33,8,128]{2,1,0:T(8,128)S(1)} %broadcast_select_fusion), channel_id=1, source_target_pairs={{0,8},{1,7},{4,12},{5,3},{8,14},{9,1},{12,10},{13,5},{14,6},{15,9}... | collective-permute-start | bytes 405512 | tf_op jit(solution)/shard_map/ppermute | solution.py:225
  19.8 0.1 copy.8.index
  20.0 1.4 %shard_map.78 = (bf16[256,1024]{1,0:T(8,128)(2,1)S(1)}, bf16[256,1024]{1,0:T(8,128)(2,1)S(1)}) custom-call(f32[256,8,128]{2,1,0:T(8,128)} %bitcast.16), custom_call_target="tpu_custom_call" | custom-call | flops 1048576 | bytes 2097152 | tf_op jit(solution)/shard_map/pallas_call | solution.py:33
  21.4 0.6 %shard_map.77 = (bf16[256,256]{1,0:T(8,128)(2,1)S(1)}, bf16[256,256]{1,0:T(8,128)(2,1)S(1)}, bf16[256,256]{1,0:T(8,128)(2,1)S(1)}, bf16[256,256]{1,0:T(8,128)(2,1)S(1)}) custom-call(s32[256,1]{1,0:T(8,128)S(1)} %copy.8.index, f32[256,256]{1,0:T(8,128)S(1)} %copy-done), custom_call_target="tpu_custom_call" | custom-call | flops 67108864 | bytes 787456 | tf_op jit(solution)/shard_map/pallas_call | solution.py:33
  22.1 1.2 %collective-permute-done.6.refs_6_ = f32[33,8,128]{2,1,0:T(8,128)S(1)} collective-permute-done((f32[33,8,128]{2,1,0:T(8,128)S(1)}, f32[33,8,128]{2,1,0:T(8,128)S(1)}, u32[]{:S(2)}, u32[]{:S(2)}) %collective-permute-start.6) | collective-permute-done | bytes 135200 | tf_op jit(solution)/shard_map/ppermute | solution.py:227
  23.3 0.8 %collective-permute-done.7.refs_7_ = f32[33,8,128]{2,1,0:T(8,128)S(1)} collective-permute-done((f32[33,8,128]{2,1,0:T(8,128)S(1)}, f32[33,8,128]{2,1,0:T(8,128)S(1)}, u32[]{:S(2)}, u32[]{:S(2)}) %collective-permute-start.7) | collective-permute-done | bytes 135200 | tf_op jit(solution)/shard_map/ppermute | solution.py:225
  24.1 1.1 %shard_map.80 = (f32[256,128]{1,0:T(8,128)S(1)}, f32[256,128]{1,0:T(8,128)S(1)}) custom-call(bf16[256,256]{1,0:T(8,128)(2,1)S(1)} %get-tuple-element.12.d_high, bf16[256,256]{1,0:T(8,128)(2,1)S(1)} %get-tuple-element.13.d_low, bf16[256,1024]{1,0:T(8,128)(2,1)S(1)} %get-tuple-element.14.m_high, bf16[256,1024]{1,0:T(8,128)(2,1)S(1)} %get-tuple-element.15.m_low, ...), custom_call_target="tpu_custom_call" | custom-call | flops 503316480 | bytes 2654208 | tf_op jit(solution)/shard_map/pallas_call | solution.py:33
  25.2 0.1 collective-permute-start.8
  25.2 0.3 shard_map.81.factor
  25.5 0.5 %collective-permute-start.9 = (f32[256,128]{1,0:T(8,128)S(1)}, f32[256,128]{1,0:T(8,128)S(1)}, u32[]{:S(2)}, u32[]{:S(2)}) collective-permute-start(f32[256,128]{1,0:T(8,128)S(1)} %shard_map.81.factor), channel_id=1, source_target_pairs={{0,1},{1,0},{2,3},{3,2},{4,5},{5,4},{6,7},{7,6},{8,9},{9,8},{10,11... | collective-permute-start | bytes 393224 | tf_op jit(solution)/shard_map/ppermute | solution.py:256
  26.1 0.5 %collective-permute-done.8.received = f32[256,128]{1,0:T(8,128)S(1)} collective-permute-done((f32[256,128]{1,0:T(8,128)S(1)}, f32[256,128]{1,0:T(8,128)S(1)}, u32[]{:S(2)}, u32[]{:S(2)}) %collective-permute-start.8) | collective-permute-done | bytes 131104 | tf_op jit(solution)/shard_map/ppermute | solution.py:265
  26.6 0.5 %collective-permute-done.9.factor_other = f32[256,128]{1,0:T(8,128)S(1)} collective-permute-done((f32[256,128]{1,0:T(8,128)S(1)}, f32[256,128]{1,0:T(8,128)S(1)}, u32[]{:S(2)}, u32[]{:S(2)}) %collective-permute-start.9) | collective-permute-done | bytes 131104 | tf_op jit(solution)/shard_map/ppermute | solution.py:256
  27.0 0.3 shard_map.82
  27.3 2.2 %collective-permute-start.10 = (f32[4,32,128]{2,1,0:T(8,128)S(1)}, f32[4,32,128]{2,1,0:T(8,128)S(1)}, u32[]{:S(2)}, u32[]{:S(2)}) collective-permute-start(f32[4,32,128]{2,1,0:T(8,128)S(1)} %dynamic-slice_bitcast_fusion), channel_id=1, source_target_pairs={{0,2},{2,0},{4,6},{6,4},{8,10},{10,8},{12,14},{14,12},{1,3},{3,1},... | collective-permute-start | bytes 196616 | tf_op jit(solution)/shard_map/ppermute | solution.py:279
  29.5 2.6 %collective-permute-done.10 = f32[4,32,128]{2,1,0:T(8,128)S(1)} collective-permute-done((f32[4,32,128]{2,1,0:T(8,128)S(1)}, f32[4,32,128]{2,1,0:T(8,128)S(1)}, u32[]{:S(2)}, u32[]{:S(2)}) %collective-permute-start.10) | collective-permute-done | bytes 65568 | tf_op jit(solution)/shard_map/ppermute | solution.py:279
  32.2 1.0 %collective-permute-start.11 = (f32[2,32,128]{2,1,0:T(8,128)S(1)}, f32[2,32,128]{2,1,0:T(8,128)S(1)}, u32[]{:S(2)}, u32[]{:S(2)}) collective-permute-start(f32[2,32,128]{2,1,0:T(8,128)S(1)} %dynamic-slice_bitcast_fusion.1), channel_id=1, source_target_pairs={{0,4},{2,6},{4,0},{6,2},{8,12},{10,14},{12,8},{14,10},{1,5},{3,7},... | collective-permute-start | bytes 98312 | tf_op jit(solution)/shard_map/ppermute | solution.py:279
  33.1 3.0 %collective-permute-done.11 = f32[2,32,128]{2,1,0:T(8,128)S(1)} collective-permute-done((f32[2,32,128]{2,1,0:T(8,128)S(1)}, f32[2,32,128]{2,1,0:T(8,128)S(1)}, u32[]{:S(2)}, u32[]{:S(2)}) %collective-permute-start.11) | collective-permute-done | bytes 32800 | tf_op jit(solution)/shard_map/ppermute | solution.py:279
  36.2 2.4 %collective-permute-start.12 = (f32[1,32,128]{2,1,0:T(8,128)S(1)}, f32[1,32,128]{2,1,0:T(8,128)S(1)}, u32[]{:S(2)}, u32[]{:S(2)}) collective-permute-start(f32[1,32,128]{2,1,0:T(8,128)S(1)} %constant_dynamic-slice_fusion), channel_id=1, source_target_pairs={{0,8},{2,10},{4,12},{6,14},{8,0},{10,2},{12,4},{14,6},{1,9},{3,11}... | collective-permute-start | bytes 49160 | tf_op jit(solution)/shard_map/ppermute | solution.py:279
  38.5 0.7 %add_negate_fusion = f32[256,128]{1,0:T(8,128)} fusion(f32[256,128]{1,0:T(8,128)S(1)} %get-tuple-element.18.keep, f32[256,128]{1,0:T(8,128)S(1)} %collective-permute-done.8.received), kind=kLoop, calls=%fused_computation | loop fusion | flops 65536 | bytes 393216 | tf_op jit(solution)/shard_map/neg | solution.py:283
  39.2 1.7 %collective-permute-done.12 = f32[1,32,128]{2,1,0:T(8,128)S(1)} collective-permute-done((f32[1,32,128]{2,1,0:T(8,128)S(1)}, f32[1,32,128]{2,1,0:T(8,128)S(1)}, u32[]{:S(2)}, u32[]{:S(2)}) %collective-permute-start.12) | collective-permute-done | bytes 16416 | tf_op jit(solution)/shard_map/ppermute | solution.py:279
  40.9 0.6 %bitcast_add_fusion.2 = f32[32,128]{1,0:T(8,128)} fusion(f32[1,32,128]{2,1,0:T(8,128)S(1)} %collective-permute-done.12, f32[2,32,128]{2,1,0:T(8,128)S(1)} %bitcast_add_fusion.1, s32[]{:T(128)S(6)} %select_n.71, f32[256,256]{1,0:T(8,128)S(1)} %copy-done, s32[]{:T(128)S(6)} %select_n.60, s32[]{:T(128)S(6)} %select_n.61), kind=kLoop, calls=%fused_computation.6 | loop fusion | flops 8192 | bytes 65548 | tf_op jit(solution)/shard_map/add | solution.py:283
  (14 shorter events, 0.1 us)
Async XLA Ops:
  1.7 1.5 %collective-permute-start = (f32[16,8,128]{2,1,0:T(8,128)S(1)}, f32[16,8,128]{2,1,0:T(8,128)S(1)}, u32[]{:S(2)}, u32[]{:S(2)}) collective-permute-start(f32[16,8,128]{2,1,0:T(8,128)S(1)} %get-tuple-element.17), channel_id=1, source_target_pairs={{0,1},{1,0},{2,3},{3,2},{4,5},{5,4},{6,7},{7,6},{8,9},{9,8},{10,11... | collective-permute-start | bytes 196616 | tf_op jit(solution)/shard_map/ppermute | solution.py:219
  3.1 6.8 %collective-permute-start.1 = (f32[33,8,128]{2,1,0:T(8,128)S(1)}, f32[33,8,128]{2,1,0:T(8,128)S(1)}, u32[]{:S(2)}, u32[]{:S(2)}) collective-permute-start(f32[33,8,128]{2,1,0:T(8,128)S(1)} %constant_dynamic-update-slice_fusion.refs_0_), channel_id=1, source_target_pairs={{0,4},{4,8},{8,12},{12,14},{14,10},{10,6},{6,2},{2,0},{1,5},{5,9},... | collective-permute-start | bytes 405512 | tf_op jit(solution)/shard_map/ppermute | solution.py:226
  6.0 5.7 %collective-permute-start.2 = (f32[33,8,128]{2,1,0:T(8,128)S(1)}, f32[33,8,128]{2,1,0:T(8,128)S(1)}, u32[]{:S(2)}, u32[]{:S(2)}) collective-permute-start(f32[33,8,128]{2,1,0:T(8,128)S(1)} %constant_dynamic-update-slice_fusion.refs_0_), channel_id=1, source_target_pairs={{4,0},{8,4},{12,8},{14,12},{10,14},{6,10},{2,6},{0,2},{5,1},{9,5},... | collective-permute-start | bytes 405512 | tf_op jit(solution)/shard_map/ppermute | solution.py:227
  9.9 5.1 %collective-permute-start.3 = (f32[33,8,128]{2,1,0:T(8,128)S(1)}, f32[33,8,128]{2,1,0:T(8,128)S(1)}, u32[]{:S(2)}, u32[]{:S(2)}) collective-permute-start(f32[33,8,128]{2,1,0:T(8,128)S(1)} %collective-permute-done.1.refs_1_), channel_id=1, source_target_pairs={{0,4},{4,8},{8,12},{12,14},{14,10},{10,6},{6,2},{2,0},{1,5},{5,9},... | collective-permute-start | bytes 405512 | tf_op jit(solution)/shard_map/ppermute | solution.py:226
  11.7 5.0 %collective-permute-start.4 = (f32[33,8,128]{2,1,0:T(8,128)S(1)}, f32[33,8,128]{2,1,0:T(8,128)S(1)}, u32[]{:S(2)}, u32[]{:S(2)}) collective-permute-start(f32[33,8,128]{2,1,0:T(8,128)S(1)} %collective-permute-done.2.refs_2_), channel_id=1, source_target_pairs={{4,0},{8,4},{12,8},{14,12},{10,14},{6,10},{2,6},{0,2},{5,1},{9,5},... | collective-permute-start | bytes 405512 | tf_op jit(solution)/shard_map/ppermute | solution.py:227
  15.0 7.1 %collective-permute-start.5 = (f32[33,8,128]{2,1,0:T(8,128)S(1)}, f32[33,8,128]{2,1,0:T(8,128)S(1)}, u32[]{:S(2)}, u32[]{:S(2)}) collective-permute-start(f32[33,8,128]{2,1,0:T(8,128)S(1)} %collective-permute-done.3.refs_3_), channel_id=1, source_target_pairs={{0,4},{4,8},{8,12},{12,14},{14,10},{10,6},{6,2},{2,0},{1,5},{5,9},... | collective-permute-start | bytes 405512 | tf_op jit(solution)/shard_map/ppermute | solution.py:226
  16.7 6.5 %collective-permute-start.6 = (f32[33,8,128]{2,1,0:T(8,128)S(1)}, f32[33,8,128]{2,1,0:T(8,128)S(1)}, u32[]{:S(2)}, u32[]{:S(2)}) collective-permute-start(f32[33,8,128]{2,1,0:T(8,128)S(1)} %collective-permute-done.4.refs_4_), channel_id=1, source_target_pairs={{4,0},{8,4},{12,8},{14,12},{10,14},{6,10},{2,6},{0,2},{5,1},{9,5},... | collective-permute-start | bytes 405512 | tf_op jit(solution)/shard_map/ppermute | solution.py:227
  17.0 2.8 %copy-start.1 = (s32[256]{0:T(256)S(1)}, s32[256]{0:T(256)}, u32[]{:S(2)}) copy-start(s32[256]{0:T(256)} %param.8) | copy-start | bytes 3076
  17.0 7.0 %collective-permute-start.7 = (f32[33,8,128]{2,1,0:T(8,128)S(1)}, f32[33,8,128]{2,1,0:T(8,128)S(1)}, u32[]{:S(2)}, u32[]{:S(2)}) collective-permute-start(f32[33,8,128]{2,1,0:T(8,128)S(1)} %broadcast_select_fusion), channel_id=1, source_target_pairs={{0,8},{1,7},{4,12},{5,3},{8,14},{9,1},{12,10},{13,5},{14,6},{15,9}... | collective-permute-start | bytes 405512 | tf_op jit(solution)/shard_map/ppermute | solution.py:225
  20.0 1.5 %copy-start = (f32[256,256]{1,0:T(8,128)S(1)}, f32[256,256]{1,0:T(8,128)}, u32[]{:S(2)}) copy-start(f32[256,256]{1,0:T(8,128)} %dinv.1) | copy-start | bytes 786436
  25.2 1.4 %collective-permute-start.8 = (f32[256,128]{1,0:T(8,128)S(1)}, f32[256,128]{1,0:T(8,128)S(1)}, u32[]{:S(2)}, u32[]{:S(2)}) collective-permute-start(f32[256,128]{1,0:T(8,128)S(1)} %get-tuple-element.19), channel_id=1, source_target_pairs={{0,1},{1,0},{2,3},{3,2},{4,5},{5,4},{6,7},{7,6},{8,9},{9,8},{10,11... | collective-permute-start | bytes 393224 | tf_op jit(solution)/shard_map/ppermute | solution.py:265
  25.5 1.5 %collective-permute-start.9 = (f32[256,128]{1,0:T(8,128)S(1)}, f32[256,128]{1,0:T(8,128)S(1)}, u32[]{:S(2)}, u32[]{:S(2)}) collective-permute-start(f32[256,128]{1,0:T(8,128)S(1)} %shard_map.81.factor), channel_id=1, source_target_pairs={{0,1},{1,0},{2,3},{3,2},{4,5},{5,4},{6,7},{7,6},{8,9},{9,8},{10,11... | collective-permute-start | bytes 393224 | tf_op jit(solution)/shard_map/ppermute | solution.py:256
  27.3 4.8 %collective-permute-start.10 = (f32[4,32,128]{2,1,0:T(8,128)S(1)}, f32[4,32,128]{2,1,0:T(8,128)S(1)}, u32[]{:S(2)}, u32[]{:S(2)}) collective-permute-start(f32[4,32,128]{2,1,0:T(8,128)S(1)} %dynamic-slice_bitcast_fusion), channel_id=1, source_target_pairs={{0,2},{2,0},{4,6},{6,4},{8,10},{10,8},{12,14},{14,12},{1,3},{3,1},... | collective-permute-start | bytes 196616 | tf_op jit(solution)/shard_map/ppermute | solution.py:279
  32.2 4.0 %collective-permute-start.11 = (f32[2,32,128]{2,1,0:T(8,128)S(1)}, f32[2,32,128]{2,1,0:T(8,128)S(1)}, u32[]{:S(2)}, u32[]{:S(2)}) collective-permute-start(f32[2,32,128]{2,1,0:T(8,128)S(1)} %dynamic-slice_bitcast_fusion.1), channel_id=1, source_target_pairs={{0,4},{2,6},{4,0},{6,2},{8,12},{10,14},{12,8},{14,10},{1,5},{3,7},... | collective-permute-start | bytes 98312 | tf_op jit(solution)/shard_map/ppermute | solution.py:279
  36.2 4.7 %collective-permute-start.12 = (f32[1,32,128]{2,1,0:T(8,128)S(1)}, f32[1,32,128]{2,1,0:T(8,128)S(1)}, u32[]{:S(2)}, u32[]{:S(2)}) collective-permute-start(f32[1,32,128]{2,1,0:T(8,128)S(1)} %constant_dynamic-slice_fusion), channel_id=1, source_target_pairs={{0,8},{2,10},{4,12},{6,14},{8,0},{10,2},{12,4},{14,6},{1,9},{3,11}... | collective-permute-start | bytes 49160 | tf_op jit(solution)/shard_map/ppermute | solution.py:279
